TPU v7x, 32 devices: a whole 2x2x4 slice. The times are simulated.
32 devices in a mesh: dp: 4 (over y, x), fsdp: 8 (over z, core).
Axes of the slice: x: 2, y: 2, z: 4, core: 2. Of those that a mesh axis runs over, the one named last changes fastest.
Arguments:
- tokens: bfloat16 [8, 512, 2048], P('fsdp', 'dp'), may hold values from -6 to 6
- attn_gain: bfloat16 [2048], P(('dp', 'fsdp')), may hold values from 0.5 to 1.5
- query_weight: bfloat16 [2048, 2048], P(('dp', 'fsdp')), may hold values from -0.125 to 0.125
- kv_weight: bfloat16 [2048, 256], P(('dp', 'fsdp')), may hold values from -0.125 to 0.125
- out_weight: bfloat16 [2048, 2048], P(('dp', 'fsdp')), may hold values from -1 to 1
- mlp_gain: bfloat16 [2048], P(('dp', 'fsdp')), may hold values from 0.5 to 1.5
- gate_weight: bfloat16 [2048, 5632], P(('dp', 'fsdp')), may hold values from -0.125 to 0.125
- up_weight: bfloat16 [2048, 5632], P(('dp', 'fsdp')), may hold values from -0.125 to 0.125
- down_weight: bfloat16 [2048, 5632], P(('dp', 'fsdp')), may hold values from -0.078125 to 0.078125
- seq_group: int32 [8], P('fsdp'), may hold values from 0 to 7
- group_weight: float32 [8], replicated, may hold values from 0.5 to 2
- out_grad: bfloat16 [8, 512, 2048], P('fsdp', 'dp'), may hold values from -6 to 6
- kv_grad: bfloat16 [8, 512, 256], P('fsdp', 'dp'), may hold values from -6 to 6
Outputs:
- layer_out: bfloat16 [8, 512, 2048], P('fsdp', 'dp')
- shared_kv: bfloat16 [8, 512, 256], P('fsdp', 'dp')
- input_grad: float32 [8, 512, 2048], P('fsdp', 'dp')
- attn_gain_grad: float32 [2048], P(('dp', 'fsdp'))
- query_weight_grad: float32 [2048, 2048], P(('dp', 'fsdp'))
- kv_weight_grad: float32 [2048, 256], P(('dp', 'fsdp'))
- out_weight_grad: float32 [2048, 2048], P(('dp', 'fsdp'))
- mlp_gain_grad: float32 [2048], P(('dp', 'fsdp'))
- gate_weight_grad: float32 [2048, 5632], P(('dp', 'fsdp'))
- up_weight_grad: float32 [2048, 5632], P(('dp', 'fsdp'))
- down_weight_grad: float32 [2048, 5632], P(('dp', 'fsdp'))
All inputs are finite; a program needn't handle non-finite values.
Results may differ from a plain program's by a relative error of at most 0.015.
Values may be sent and summed in bfloat16 or wider, within the bound.
No kernel may reach another device: no remote copies, remote signals or barrier semaphores. Data moves between devices by JAX's collectives and lax.ppermute only.
A program may use at most 512 MiB of HBM per device.

v0:
```python
import jax
import jax.numpy as jnp
from jax import lax
from jax.sharding import PartitionSpec as P

norm_eps = 1e-05
rope_base = 10000.0
masked_score = -1e30


def rope_tables(positions, half_width):
    index_vec = jnp.arange(half_width, dtype=jnp.float32)
    frequency = jnp.power(rope_base, -(2.0 * index_vec) / (2 * half_width))
    angles = positions.astype(jnp.float32)[:, None] * frequency[None, :]
    return (jnp.cos(angles), jnp.sin(angles))


def rotate(values, cos_vals, sin_vals):
    half_width = values.shape[-1] // 2
    first_half = values[..., :half_width]
    second_half = values[..., half_width:]
    return jnp.concatenate(
        [
            first_half * cos_vals - second_half * sin_vals,
            second_half * cos_vals + first_half * sin_vals,
        ],
        axis=-1,
    )


def rotate_back(values, cos_vals, sin_vals):
    half_width = values.shape[-1] // 2
    first_half = values[..., :half_width]
    second_half = values[..., half_width:]
    return jnp.concatenate(
        [
            first_half * cos_vals + second_half * sin_vals,
            second_half * cos_vals - first_half * sin_vals,
        ],
        axis=-1,
    )


def norm_back(grad_hat, normed_hat, inv_rms):
    inner_mean = jnp.mean(grad_hat * normed_hat, axis=1, keepdims=True)
    return inv_rms * (grad_hat - normed_hat * inner_mean)


def project_step(normed_hat, running, pieces):
    normed = (normed_hat * pieces[0].astype(jnp.float32)[None, :]).astype(jnp.bfloat16)
    outputs = [normed]
    for summed, matrix in zip(running[1:], pieces[1:]):
        outputs.append(jnp.dot(normed, matrix, preferred_element_type=jnp.float32))
    return tuple(outputs)


def return_step(grads_left, pieces):
    piece_rows = pieces[0].shape[0]
    columns = jnp.zeros((grads_left[0].shape[0], piece_rows), jnp.float32)
    for grad_part, matrix in zip(grads_left, pieces[1:]):
        columns = columns + lax.dot_general(
            grad_part, matrix, (((1,), (1,)), ((), ())), preferred_element_type=jnp.float32
        )
    gain_full = pieces[0].astype(jnp.float32)
    return (columns, gain_full)


def contract_step(left_rows, block_piece):
    return jnp.dot(left_rows, block_piece, preferred_element_type=jnp.float32)


def expand_map(left_rows, block_piece):
    return lax.dot_general(
        left_rows, block_piece, (((1,), (1,)), ((), ())), preferred_element_type=jnp.float32
    )


def local(
    tokens,
    attn_gain,
    query_weight,
    kv_weight,
    out_weight,
    mlp_gain,
    gate_weight,
    up_weight,
    down_weight,
    seq_group,
    group_weight,
    out_grad,
    kv_grad,
):
    inputs = tokens[0].astype(jnp.float32)
    tok_rows = inputs.shape[0]
    model_width = inputs.shape[1]
    head_width = kv_weight.shape[1] // 2
    query_width = query_weight.shape[1]
    head_count = query_width // head_width
    ff_width = gate_weight.shape[1]
    score_scale = head_width ** (-0.5)
    first_pos = lax.axis_index("dp") * tok_rows
    positions = first_pos + jnp.arange(tok_rows, dtype=jnp.int32)
    cos_vals, sin_vals = rope_tables(positions, head_width // 2)
    inv_one = lax.rsqrt(jnp.mean(inputs * inputs, axis=1, keepdims=True) + norm_eps)
    hat_one = inputs * inv_one
    start_one = (
        jnp.zeros((tok_rows, model_width), jnp.bfloat16),
        jnp.zeros((tok_rows, query_width), jnp.float32),
        jnp.zeros((tok_rows, 2 * head_width), jnp.float32),
    )
    normed_one, query_pre, kv_pre = project_step(
        hat_one,
        start_one,
        (
            lax.all_gather(attn_gain, ("dp", "fsdp"), axis=0, tiled=True),
            lax.all_gather(query_weight, ("dp", "fsdp"), axis=0, tiled=True),
            lax.all_gather(kv_weight, ("dp", "fsdp"), axis=0, tiled=True),
        ),
    )
    query_rot = rotate(
        query_pre.reshape(tok_rows, head_count, head_width),
        cos_vals[:, None, :],
        sin_vals[:, None, :],
    )
    queries = (query_rot * score_scale).astype(jnp.bfloat16)
    key_rot = rotate(kv_pre[:, :head_width], cos_vals, sin_vals)
    shared = jnp.concatenate([key_rot, kv_pre[:, head_width:]], axis=1).astype(jnp.bfloat16)
    all_keys = lax.all_gather(shared, "dp", axis=0, tiled=True)
    seq_len = all_keys.shape[0]
    block_len = min(512, seq_len)
    block_count = (first_pos + tok_rows + block_len - 1) // block_len

    def block_scores(block_index):
        block_kv = lax.dynamic_slice_in_dim(all_keys, block_index * block_len, block_len, 0)
        scores = jnp.einsum(
            "thd,kd->thk", queries, block_kv[:, :head_width], preferred_element_type=jnp.float32
        )
        key_pos = block_index * block_len + jnp.arange(block_len, dtype=jnp.int32)
        visible = key_pos[None, :] <= positions[:, None]
        return (jnp.where(visible[:, None, :], scores, masked_score), block_kv)

    def max_pass(block_index, running):
        row_peak, row_total = running
        scores, block_kv = block_scores(block_index)
        new_peak = jnp.maximum(row_peak, jnp.max(scores, axis=2))
        row_total = row_total * jnp.exp(row_peak - new_peak) + jnp.sum(
            jnp.exp(scores - new_peak[:, :, None]), axis=2
        )
        return (new_peak, row_total)

    start_peak = (
        jnp.full((tok_rows, head_count), masked_score, jnp.float32),
        jnp.zeros((tok_rows, head_count), jnp.float32),
    )
    row_peak, row_total = lax.fori_loop(0, block_count, max_pass, start_peak)
    log_total = row_peak + jnp.log(row_total)

    def value_pass(block_index, attended):
        scores, block_kv = block_scores(block_index)
        prob_vals = jnp.exp(scores - log_total[:, :, None]).astype(jnp.bfloat16)
        return attended + jnp.einsum(
            "thk,kd->thd", prob_vals, block_kv[:, head_width:], preferred_element_type=jnp.float32
        )

    attended = lax.fori_loop(
        0, block_count, value_pass, jnp.zeros((tok_rows, head_count, head_width), jnp.float32)
    )
    attn_rows = attended.reshape(tok_rows, query_width).astype(jnp.bfloat16)
    attn_branch = expand_map(
        attn_rows, lax.all_gather(out_weight, ("dp", "fsdp"), axis=0, tiled=True)
    )
    middle = inputs + attn_branch
    inv_two = lax.rsqrt(jnp.mean(middle * middle, axis=1, keepdims=True) + norm_eps)
    hat_two = middle * inv_two
    start_two = (
        jnp.zeros((tok_rows, model_width), jnp.bfloat16),
        jnp.zeros((tok_rows, ff_width), jnp.float32),
        jnp.zeros((tok_rows, ff_width), jnp.float32),
    )
    normed_two, gate_pre, up_pre = project_step(
        hat_two,
        start_two,
        (
            lax.all_gather(mlp_gain, ("dp", "fsdp"), axis=0, tiled=True),
            lax.all_gather(gate_weight, ("dp", "fsdp"), axis=0, tiled=True),
            lax.all_gather(up_weight, ("dp", "fsdp"), axis=0, tiled=True),
        ),
    )
    sigmoid_gate = jax.nn.sigmoid(gate_pre)
    silu_gate = gate_pre * sigmoid_gate
    hidden = (silu_gate * up_pre).astype(jnp.bfloat16)
    mlp_branch = expand_map(hidden, lax.all_gather(down_weight, ("dp", "fsdp"), axis=0, tiled=True))
    layer_out = (middle + mlp_branch).astype(jnp.bfloat16)
    group_ids = jnp.arange(group_weight.shape[0], dtype=jnp.int32)
    seq_weight = jnp.sum(jnp.where(group_ids == seq_group[0], group_weight, 0.0))
    grad_out = out_grad[0].astype(jnp.float32) * seq_weight
    grad_out_low = grad_out.astype(jnp.bfloat16)
    grad_hidden = contract_step(
        grad_out_low, lax.all_gather(down_weight, ("dp", "fsdp"), axis=0, tiled=True)
    )
    grad_gate = (
        grad_hidden * up_pre * sigmoid_gate * (1.0 + gate_pre * (1.0 - sigmoid_gate))
    ).astype(jnp.bfloat16)
    grad_up = (grad_hidden * silu_gate).astype(jnp.bfloat16)
    grad_normed_two, gain_two = return_step(
        (grad_gate, grad_up),
        (
            lax.all_gather(mlp_gain, ("dp", "fsdp"), axis=0, tiled=True),
            lax.all_gather(gate_weight, ("dp", "fsdp"), axis=0, tiled=True),
            lax.all_gather(up_weight, ("dp", "fsdp"), axis=0, tiled=True),
        ),
    )
    grad_middle = grad_out + norm_back(grad_normed_two * gain_two[None, :], hat_two, inv_two)
    grad_mid_low = grad_middle.astype(jnp.bfloat16)
    lead_dims = (((0,), (0,)), ((), ()))
    mlp_shares = lax.psum_scatter(
        jnp.concatenate(
            [
                lax.dot_general(
                    normed_two, grad_gate, lead_dims, preferred_element_type=jnp.float32
                ),
                lax.dot_general(normed_two, grad_up, lead_dims, preferred_element_type=jnp.float32),
                lax.dot_general(
                    grad_out_low, hidden, lead_dims, preferred_element_type=jnp.float32
                ),
            ],
            axis=1,
        ),
        ("dp", "fsdp"),
        scatter_dimension=0,
        tiled=True,
    )
    grad_attn = contract_step(
        grad_mid_low, lax.all_gather(out_weight, ("dp", "fsdp"), axis=0, tiled=True)
    )
    grad_heads = grad_attn.astype(jnp.bfloat16).reshape(tok_rows, head_count, head_width)
    row_dot = jnp.sum(grad_heads.astype(jnp.float32) * attended, axis=2)

    def grad_pass(block_index, running):
        grad_query, grad_kv = running
        scores, block_kv = block_scores(block_index)
        prob_vals = jnp.exp(scores - log_total[:, :, None])
        probs_low = prob_vals.astype(jnp.bfloat16)
        grad_probs = jnp.einsum(
            "thd,kd->thk", grad_heads, block_kv[:, head_width:], preferred_element_type=jnp.float32
        )
        grad_scores = (prob_vals * (grad_probs - row_dot[:, :, None])).astype(jnp.bfloat16)
        grad_query = grad_query + jnp.einsum(
            "thk,kd->thd", grad_scores, block_kv[:, :head_width], preferred_element_type=jnp.float32
        )
        grad_keys = jnp.einsum(
            "thk,thd->kd", grad_scores, queries, preferred_element_type=jnp.float32
        )
        grad_values = jnp.einsum(
            "thk,thd->kd", probs_low, grad_heads, preferred_element_type=jnp.float32
        )
        grad_kv = lax.dynamic_update_slice_in_dim(
            grad_kv, jnp.concatenate([grad_keys, grad_values], axis=1), block_index * block_len, 0
        )
        return (grad_query, grad_kv)

    start_grad = (
        jnp.zeros((tok_rows, head_count, head_width), jnp.float32),
        jnp.zeros((seq_len, 2 * head_width), jnp.float32),
    )
    grad_query, grad_kv = lax.fori_loop(0, block_count, grad_pass, start_grad)
    kv_total = lax.psum_scatter(
        grad_kv.astype(jnp.bfloat16), "dp", scatter_dimension=0, tiled=True
    ).astype(jnp.float32) + kv_grad[0].astype(jnp.float32)
    key_back = rotate_back(kv_total[:, :head_width], cos_vals, sin_vals)
    grad_kv_pre = jnp.concatenate([key_back, kv_total[:, head_width:]], axis=1).astype(jnp.bfloat16)
    query_back = rotate_back(grad_query * score_scale, cos_vals[:, None, :], sin_vals[:, None, :])
    grad_query_pre = query_back.reshape(tok_rows, query_width).astype(jnp.bfloat16)
    grad_normed_one, gain_one = return_step(
        (grad_query_pre, grad_kv_pre),
        (
            lax.all_gather(attn_gain, ("dp", "fsdp"), axis=0, tiled=True),
            lax.all_gather(query_weight, ("dp", "fsdp"), axis=0, tiled=True),
            lax.all_gather(kv_weight, ("dp", "fsdp"), axis=0, tiled=True),
        ),
    )
    input_grad = grad_middle + norm_back(grad_normed_one * gain_one[None, :], hat_one, inv_one)
    attn_shares = (
        lax.psum_scatter(
            jnp.sum(grad_normed_one * hat_one, axis=0),
            ("dp", "fsdp"),
            scatter_dimension=0,
            tiled=True,
        ),
        lax.psum_scatter(
            jnp.sum(grad_normed_two * hat_two, axis=0),
            ("dp", "fsdp"),
            scatter_dimension=0,
            tiled=True,
        ),
        lax.psum_scatter(
            lax.dot_general(
                normed_one, grad_query_pre, lead_dims, preferred_element_type=jnp.float32
            ),
            ("dp", "fsdp"),
            scatter_dimension=0,
            tiled=True,
        ),
        lax.psum_scatter(
            lax.dot_general(normed_one, grad_kv_pre, lead_dims, preferred_element_type=jnp.float32),
            ("dp", "fsdp"),
            scatter_dimension=0,
            tiled=True,
        ),
        lax.psum_scatter(
            lax.dot_general(grad_mid_low, attn_rows, lead_dims, preferred_element_type=jnp.float32),
            ("dp", "fsdp"),
            scatter_dimension=0,
            tiled=True,
        ),
    )
    return (
        layer_out[None],
        shared[None],
        input_grad[None],
        attn_shares[0],
        attn_shares[2],
        attn_shares[3],
        attn_shares[4],
        attn_shares[1],
        mlp_shares[:, :ff_width],
        mlp_shares[:, ff_width : 2 * ff_width],
        mlp_shares[:, 2 * ff_width :],
    )


def solution(mesh):
    return jax.shard_map(
        local,
        mesh=mesh,
        in_specs=(
            P("fsdp", "dp", None),
            P(("dp", "fsdp")),
            P(("dp", "fsdp"), None),
            P(("dp", "fsdp"), None),
            P(("dp", "fsdp"), None),
            P(("dp", "fsdp")),
            P(("dp", "fsdp"), None),
            P(("dp", "fsdp"), None),
            P(("dp", "fsdp"), None),
            P("fsdp"),
            P(),
            P("fsdp", "dp", None),
            P("fsdp", "dp", None),
        ),
        out_specs=(
            P("fsdp", "dp", None),
            P("fsdp", "dp", None),
            P("fsdp", "dp", None),
            P(("dp", "fsdp")),
            P(("dp", "fsdp"), None),
            P(("dp", "fsdp"), None),
            P(("dp", "fsdp"), None),
            P(("dp", "fsdp")),
            P(("dp", "fsdp"), None),
            P(("dp", "fsdp"), None),
            P(("dp", "fsdp"), None),
        ),
        check_vma=False,
    )
```

profile of v0, /device:TPU:0, one launch (start us, length us, event | category | flops | bytes accessed | tf_op | source)
XLA Modules:
  0.0 3316.1 jit_solution(6291260119929494556)
XLA Ops:
  12.9 42.1 %all-reduce.6 = (bf16[2048]{0:T(1024)(128)(2,1)S(1)}, bf16[2048]{0:T(1024)(128)(2,1)S(1)}) all-reduce(bf16[2048]{0:T(1024)(128)(2,1)S(1)} %dynamic-update-slice, bf16[2048]{0:T(1024)(128)(2,1)S(1)} %dynamic-update-slice.1), channel_id=1, replica_groups=mesh['dp'=4,'fsdp'=8] {'dp','fsdp'}, use_global_device_ids=true, to_apply=%add | all-reduce | flops 4096 | bytes 16384
  58.3 9.4 all-gather.7.cloned.1.call-done
  70.3 8.9 all_gather.37
  79.3 67.4 %all-gather.9.cloned.1.call-done = bf16[2048,2048]{1,0:T(8,128)(2,1)} async-done(((bf16[64,2048]{1,0:T(8,128)(2,1)}), bf16[2048,2048]{1,0:T(8,128)(2,1)}) %all-gather.9.cloned.1.call-update) | async-done | bytes 8388624 | tf_op jit(solution)/shard_map/all_gather | solution.py:116
  146.7 12.4 copy.49
  159.1 5.8 fusion.55
  171.1 54.3 %all-gather.11.cloned.1.call-done = bf16[2048,2048]{1,0:T(8,128)(2,1)} async-done(((bf16[64,2048]{1,0:T(8,128)(2,1)}), bf16[2048,2048]{1,0:T(8,128)(2,1)}) %all-gather.11.cloned.1.call-update) | async-done | bytes 8388624 | tf_op jit(solution)/shard_map/all_gather | solution.py:170
  225.4 6.5 multiply_reduce_fusion.3
  232.1 138.6 %all-gather.13.cloned.1.call-done = bf16[2048,5632]{1,0:T(8,128)(2,1)} async-done(((bf16[64,5632]{1,0:T(8,128)(2,1)}), bf16[2048,5632]{1,0:T(8,128)(2,1)}) %all-gather.13.cloned.1.call-update) | async-done | bytes 23068688 | tf_op jit(solution)/shard_map/all_gather | solution.py:185
  370.7 12.3 fusion.90
  383.0 132.5 %all-gather.15.cloned.1.call-done = bf16[2048,5632]{1,0:T(8,128)(2,1)} async-done(((bf16[64,5632]{1,0:T(8,128)(2,1)}), bf16[2048,5632]{1,0:T(8,128)(2,1)}) %all-gather.15.cloned.1.call-update) | async-done | bytes 23068688 | tf_op jit(solution)/shard_map/all_gather | solution.py:186
  515.5 12.3 fusion.91
  527.8 132.5 %all-gather.17.cloned.1.call-done = bf16[2048,5632]{1,0:T(8,128)(2,1)} async-done(((bf16[64,5632]{1,0:T(8,128)(2,1)}), bf16[2048,5632]{1,0:T(8,128)(2,1)}) %all-gather.17.cloned.1.call-update) | async-done | bytes 23068688 | tf_op jit(solution)/shard_map/all_gather | solution.py:192
  660.3 15.5 multiply_convert_fusion.1
  675.8 17.9 fusion.95
  693.7 17.8 fusion.94
  711.5 13.0 fusion.92
  724.4 14.2 multiply_reduce_fusion
  740.9 5.1 convolution_convert_fusion
  747.7 9.2 while.39
  758.8 19.9 fusion.59
  778.7 88.6 %pad_maximum_fusion.1 = f32[2048,16896]{1,0:T(8,128)} fusion(f32[2048,5632]{1,0:T(8,128)} %fusion.59, f32[2048,5632]{1,0:T(8,128)} %fusion.95, f32[2048,5632]{1,0:T(8,128)} %fusion.94), kind=kLoop, calls=%fused_computation.45 | loop fusion | flops 69206016 | bytes 276824064 | tf_op jit(solution)/shard_map/concatenate | solution.py:217
  872.4 8.5 fusion.57
  882.2 8.3 fusion.61
  892.1 6.6 fusion.93
  898.8 12.9 fusion.37
  914.4 40.1 %all-reduce.5 = (f32[2048]{0:T(1024)S(1)}, f32[2048]{0:T(1024)S(1)}) all-reduce(f32[2048]{0:T(1024)S(1)} %get-tuple-element.279, f32[2048]{0:T(1024)S(1)} %copy-done.23), channel_id=3, replica_groups=mesh['dp'=4,'fsdp'=8] {'dp','fsdp'}, use_global_device_ids=true, to_apply=%region_16.17.clone | all-reduce | flops 4096 | bytes 32768
  958.3 1835.2 %all-reduce.9.cloned.1.call-done = f32[2048,16896]{1,0:T(8,128)} async-done(((f32[2048,16896]{1,0:T(8,128)}), f32[2048,16896]{1,0:T(8,128)}) %all-reduce.9.cloned.1.call-update) | async-done | bytes 138412048
  2793.5 5.1 fusion.89
  2798.6 137.7 %reduce-scatter.9.cloned.1.call-done = f32[64,256]{1,0:T(8,128)} async-done(((f32[2048,256]{1,0:T(8,128)}), f32[64,256]{1,0:T(8,128)}) %reduce-scatter.9.cloned.1.call-update) | async-done | bytes 65552 | tf_op jit(solution)/shard_map/reduce_scatter | solution.py:304
  2936.2 185.6 %reduce-scatter.7.cloned.1.call-done = f32[64,2048]{1,0:T(8,128)} async-done(((f32[2048,2048]{1,0:T(8,128)}), f32[64,2048]{1,0:T(8,128)}) %reduce-scatter.7.cloned.1.call-update) | async-done | bytes 524304 | tf_op jit(solution)/shard_map/reduce_scatter | solution.py:296
  3121.9 187.2 %reduce-scatter.11.cloned.1.call-done = f32[64,2048]{1,0:T(8,128)} async-done(((f32[2048,2048]{1,0:T(8,128)}), f32[64,2048]{1,0:T(8,128)}) %reduce-scatter.11.cloned.1.call-update) | async-done | bytes 524304 | tf_op jit(solution)/shard_map/reduce_scatter | solution.py:310
  (156 shorter events, 50.1 us)
Async XLA Ops:
  7.2 60.5 %all-gather.7.cloned.1.call-start = ((), (), s32[]{:S(2)}) async-start(), calls=%async_computation.4 | async-start | bytes 1081344 | tf_op jit(solution)/shard_map/all_gather | solution.py:117
  7.9 138.8 %all-gather.9.cloned.1.call-start = ((), (), s32[]{:S(2)}) async-start(), calls=%async_computation.5 | async-start | bytes 8650752 | tf_op jit(solution)/shard_map/all_gather | solution.py:116
  8.7 216.8 %all-gather.11.cloned.1.call-start = ((), (), s32[]{:S(2)}) async-start(), calls=%async_computation.6 | async-start | bytes 8650752 | tf_op jit(solution)/shard_map/all_gather | solution.py:170
  9.4 361.3 %all-gather.13.cloned.1.call-start = ((), (), s32[]{:S(2)}) async-start(), calls=%async_computation.7 | async-start | bytes 23789568 | tf_op jit(solution)/shard_map/all_gather | solution.py:185
  10.0 505.5 %all-gather.15.cloned.1.call-start = ((), (), s32[]{:S(2)}) async-start(), calls=%async_computation.8 | async-start | bytes 23789568 | tf_op jit(solution)/shard_map/all_gather | solution.py:186
  10.6 649.8 %all-gather.17.cloned.1.call-start = ((), (), s32[]{:S(2)}) async-start(), calls=%async_computation.9 | async-start | bytes 23789568 | tf_op jit(solution)/shard_map/all_gather | solution.py:192
  11.1 856.4 %reduce-scatter.5.cloned.1.call-start = ((), (), s32[]{:S(2)}) async-start(), calls=%async_computation.10 | async-start | bytes 327680 | tf_op jit(solution)/shard_map/reduce_scatter | solution.py:267
  55.0 104.1 %copy-start.11 = (f32[2048]{0:T(1024)}, f32[2048]{0:T(1024)S(1)}, u32[]{:S(2)}) copy-start(f32[2048]{0:T(1024)S(1)} %convert_element_type.119) | copy-start | bytes 24580
  55.7 14.1 copy-start.26
  55.7 14.1 copy-start.28
  58.3 100.9 %copy-start.24 = (f32[128]{0:T(128)}, f32[128]{0:T(128)S(1)}, u32[]{:S(2)}) copy-start(f32[128]{0:T(128)S(1)} %add_rsqrt_fusion.1) | copy-start | bytes 1540
  70.0 89.1 %copy-start.17 = (bf16[128,64]{1,0:T(8,128)(2,1)}, bf16[128,64]{1,0:T(8,128)(2,1)S(1)}, u32[]{:S(2)}) copy-start(bf16[128,64]{1,0:T(8,128)(2,1)S(1)} %get-tuple-element.351) | copy-start | bytes 49156
  70.0 89.1 %copy-start.19 = (bf16[128,64]{1,0:T(8,128)(2,1)}, bf16[128,64]{1,0:T(8,128)(2,1)S(1)}, u32[]{:S(2)}) copy-start(bf16[128,64]{1,0:T(8,128)(2,1)S(1)} %get-tuple-element.352) | copy-start | bytes 49156
  70.1 94.8 %copy-start.13 = (f32[128,64]{0,1:T(8,128)}, f32[128,64]{0,1:T(8,128)S(1)}, u32[]{:S(2)}) copy-start(f32[128,64]{0,1:T(8,128)S(1)} %copy.51) | copy-start | bytes 98308
  70.2 94.8 %copy-start.15 = (f32[128,64]{0,1:T(8,128)}, f32[128,64]{0,1:T(8,128)S(1)}, u32[]{:S(2)}) copy-start(f32[128,64]{0,1:T(8,128)S(1)} %copy.50) | copy-start | bytes 98308
  146.7 12.4 copy-start.1
  232.0 506.7 %copy-start.3 = (f32[128,2048]{1,0:T(8,128)}, f32[128,2048]{1,0:T(8,128)S(1)}, u32[]{:S(2)}) copy-start(f32[128,2048]{1,0:T(8,128)S(1)} %get-tuple-element.354) | copy-start | bytes 3145732
  724.4 14.2 copy-start.9
  740.9 5.1 copy-start.5
  747.7 11.1 copy-start.10
  750.5 4.1 copy-start
  758.7 2034.7 %all-reduce.9.cloned.1.call-start = ((), (), s32[]{:S(2)}) async-start(), calls=%async_computation.14 | async-start | bytes 276824064
  867.4 2.0 copy-start.2
  867.4 2.0 copy-start.12
  867.5 2068.8 %reduce-scatter.9.cloned.1.call-start = ((), (), s32[]{:S(2)}) async-start(), calls=%async_computation.12 | async-start | bytes 2162688 | tf_op jit(solution)/shard_map/reduce_scatter | solution.py:304
  869.5 2.7 copy-start.14
  869.5 2.7 copy-start.16
  871.4 2250.5 %reduce-scatter.7.cloned.1.call-start = ((), (), s32[]{:S(2)}) async-start(), calls=%async_computation.11 | async-start | bytes 17301504 | tf_op jit(solution)/shard_map/reduce_scatter | solution.py:296
  880.9 2428.2 %reduce-scatter.11.cloned.1.call-start = ((), (), s32[]{:S(2)}) async-start(), calls=%async_computation.13 | async-start | bytes 17301504 | tf_op jit(solution)/shard_map/reduce_scatter | solution.py:310
  892.1 6.6 copy-start.4
  892.1 6.6 copy-start.7
  898.8 15.6 copy-start.23
  (9 other events, 11.3 us)
Sparse Core Ops, SparseCore 0:
  11.0 56.6 all-gather.6
  70.6 76.0 all-gather.8
  149.7 75.7 all-gather.10
  228.2 142.5 all-gather.12
  373.4 142.0 all-gather.14
  518.2 142.0 all-gather.16
  758.9 22.4 reduce-scatter.4
  867.6 1925.8 all-reduce.8
  2796.3 139.8 reduce-scatter.8
  2938.9 182.8 reduce-scatter.6
  3124.7 184.3 reduce-scatter.10
where the time goes:
time: 3320 us
  waiting for transfers between devices  2880 us (87%)
  matrix products  193 us (6%)
  other arithmetic  102 us (3%)
  blocking collectives  91.1 us (3%)
    unnamed x12, waiting for transfers between devices  1840 us
    reduce_scatter x1, waiting for transfers between devices, local(): lax.psum_scatter(lax.dot_general(grad_mid_low, attn_rows, lead_dims, pref...  187 us
    reduce_scatter x1, waiting for transfers between devices, local(): lax.psum_scatter(lax.dot_general(normed_one, grad_query_pre, lead_dims, p...  186 us
    all_gather x1, waiting for transfers between devices, local(): lax.all_gather(gate_weight, ('dp', 'fsdp'), axis=0, tiled=True)  139 us
    reduce_scatter x1, waiting for transfers between devices, local(): lax.psum_scatter(lax.dot_general(normed_one, grad_kv_pre, lead_dims, pref...  138 us
    all_gather x1, waiting for transfers between devices, local(): lax.all_gather(down_weight, ('dp', 'fsdp'), axis=0, tiled=True)  133 us
    all_gather x1, waiting for transfers between devices, local(): lax.all_gather(up_weight, ('dp', 'fsdp'), axis=0, tiled=True)  132 us
    concatenate x1, other arithmetic, local(): jnp.concatenate([lax.dot_general(normed_two, grad_gate, lead_dims, prefer...  88.6 us
  transfers between devices with their start and end apart: 11, of which 10 were waited for; matrix products, arithmetic and copies ran while one was open for 7% of the time, Pallas kernels for 0%

commit v1 on v0

v1 whole, which is shorter than its diff:
```python
import jax
import jax.numpy as jnp
from jax import lax
from jax.sharding import PartitionSpec as P

norm_eps = 1e-05
rope_base = 10000.0
masked_score = -1e30
f32 = jnp.float32
bf16 = jnp.bfloat16


def rope_tables(positions, half_width):
    index_vec = jnp.arange(half_width, dtype=f32)
    frequency = jnp.power(rope_base, -(2.0 * index_vec) / (2 * half_width))
    angles = positions.astype(f32)[:, None] * frequency[None, :]
    return (jnp.cos(angles), jnp.sin(angles))


def rotate(values, cos_vals, sin_vals):
    half_width = values.shape[-1] // 2
    first_half = values[..., :half_width]
    second_half = values[..., half_width:]
    return jnp.concatenate(
        [
            first_half * cos_vals - second_half * sin_vals,
            second_half * cos_vals + first_half * sin_vals,
        ],
        axis=-1,
    )


def rotate_back(values, cos_vals, sin_vals):
    return rotate(values, cos_vals, -sin_vals)


def norm_back(grad_hat, normed_hat, inv_rms):
    inner_mean = jnp.mean(grad_hat * normed_hat, axis=1, keepdims=True)
    return inv_rms * (grad_hat - normed_hat * inner_mean)


def mm(left, right):
    return jnp.dot(left, right, preferred_element_type=f32)


def mm_nt(left, right):
    return lax.dot_general(left, right, (((1,), (1,)), ((), ())), preferred_element_type=f32)


def mm_tn(left, right):
    return lax.dot_general(left, right, (((0,), (0,)), ((), ())), preferred_element_type=f32)


def local(
    tokens,
    attn_gain,
    query_weight,
    kv_weight,
    out_weight,
    mlp_gain,
    gate_weight,
    up_weight,
    down_weight,
    seq_group,
    group_weight,
    out_grad,
    kv_grad,
):
    dp_size = lax.axis_size("dp")
    fsdp_size = lax.axis_size("fsdp")
    dp_index = lax.axis_index("dp")
    tok_rows, model_width = tokens.shape[1:]
    own_rows = query_weight.shape[0]
    head_width = kv_weight.shape[1] // 2
    kv_width = 2 * head_width
    query_cols = query_weight.shape[1] // dp_size
    head_count = query_cols // head_width
    ff_cols = gate_weight.shape[1] // dp_size
    score_scale = head_width ** (-0.5)

    def permuted(rows):
        blocks = rows.reshape(rows.shape[0], dp_size, fsdp_size, own_rows)
        return blocks.transpose(0, 2, 1, 3).reshape(rows.shape)

    def unpermuted(rows):
        blocks = rows.reshape(rows.shape[0], fsdp_size, dp_size, own_rows)
        return blocks.transpose(0, 2, 1, 3).reshape(rows.shape)

    def peers(step):
        return [(i, i ^ step) for i in range(dp_size)]

    def gathered(block):
        blocks = [block] + [lax.ppermute(block, "dp", peers(k)) for k in range(1, dp_size)]
        return jnp.concatenate(blocks, axis=0)

    def scattered(partial):
        rows = partial.shape[0] // dp_size
        total = partial[:rows]
        for k in range(1, dp_size):
            part = partial[k * rows : (k + 1) * rows].astype(bf16)
            total = total + lax.ppermute(part, "dp", peers(k)).astype(f32)
        return total

    def column_blocks(matrix):
        cols = matrix.shape[1] // dp_size
        return matrix.reshape(own_rows, dp_size, cols).transpose(1, 0, 2)

    def exchanged(packed):
        return lax.all_to_all(packed, "dp", 0, 0)

    def all_rows(packed):
        return lax.all_gather(
            packed.reshape(dp_size * own_rows, packed.shape[2]), "fsdp", axis=0, tiled=True
        )

    def own_share(grads):
        share = lax.psum_scatter(grads.astype(bf16), "fsdp", scatter_dimension=0, tiled=True)
        return exchanged(share.reshape(dp_size, own_rows, grads.shape[1])).astype(f32)

    def joined(blocks):
        return blocks.transpose(1, 0, 2).reshape(own_rows, dp_size * blocks.shape[2])

    gain_one = attn_gain.astype(f32)[:, None]
    gain_two = mlp_gain.astype(f32)[:, None]

    def scaled(matrix, gain):
        return (matrix.astype(f32) * gain).astype(bf16)

    attn_pack = jnp.concatenate(
        [
            column_blocks(scaled(query_weight, gain_one)),
            jnp.broadcast_to(scaled(kv_weight, gain_one)[None], (dp_size, own_rows, kv_width)),
            column_blocks(out_weight),
        ],
        axis=2,
    )
    ff_pack = jnp.concatenate(
        [
            column_blocks(scaled(gate_weight, gain_two)),
            column_blocks(scaled(up_weight, gain_two)),
        ],
        axis=2,
    )
    attn_all = all_rows(exchanged(attn_pack))
    ff_all = all_rows(exchanged(ff_pack))
    down_all = all_rows(exchanged(column_blocks(down_weight)))
    query_all = attn_all[:, :query_cols]
    kv_all = attn_all[:, query_cols : query_cols + kv_width]
    out_all = attn_all[:, query_cols + kv_width :]

    def block_positions(k):
        return (dp_index ^ k) * tok_rows + jnp.arange(tok_rows, dtype=jnp.int32)

    positions = jnp.concatenate([block_positions(k) for k in range(dp_size)])
    cos_all, sin_all = rope_tables(positions, head_width // 2)
    cos_own, sin_own = cos_all[:tok_rows], sin_all[:tok_rows]
    seq_len = positions.shape[0]

    inputs = permuted(tokens[0]).astype(f32)
    inv_one = lax.rsqrt(jnp.mean(inputs * inputs, axis=1, keepdims=True) + norm_eps)
    hat_one = inputs * inv_one
    hat_one_low = hat_one.astype(bf16)
    hat_one_seq = gathered(hat_one_low)
    kv_pre = mm(hat_one_low, kv_all)
    key_rot = rotate(kv_pre[:, :head_width], cos_own, sin_own)
    shared = jnp.concatenate([key_rot, kv_pre[:, head_width:]], axis=1).astype(bf16)
    shared_seq = gathered(shared)
    keys, values = shared_seq[:, :head_width], shared_seq[:, head_width:]
    query_pre = mm(hat_one_seq, query_all).reshape(seq_len, head_count, head_width)
    query_rot = rotate(query_pre, cos_all[:, None, :], sin_all[:, None, :])
    queries = (query_rot * score_scale).astype(bf16)
    scores = jnp.einsum("thd,kd->htk", queries, keys, preferred_element_type=f32)
    visible = positions[None, :] <= positions[:, None]
    scores = jnp.where(visible[None], scores, masked_score)
    probs = jax.nn.softmax(scores, axis=-1)
    probs_low = probs.astype(bf16)
    attended = jnp.einsum("htk,kd->thd", probs_low, values, preferred_element_type=f32)
    attn_rows = attended.reshape(seq_len, query_cols).astype(bf16)
    middle = inputs + scattered(mm_nt(attn_rows, out_all))

    inv_two = lax.rsqrt(jnp.mean(middle * middle, axis=1, keepdims=True) + norm_eps)
    hat_two = middle * inv_two
    hat_two_seq = gathered(hat_two.astype(bf16))
    pre = mm(hat_two_seq, ff_all)
    gate_pre, up_pre = pre[:, :ff_cols], pre[:, ff_cols:]
    sigmoid_gate = jax.nn.sigmoid(gate_pre)
    silu_gate = gate_pre * sigmoid_gate
    hidden = (silu_gate * up_pre).astype(bf16)
    layer_out = unpermuted((middle + scattered(mm_nt(hidden, down_all))).astype(bf16))

    group_ids = jnp.arange(group_weight.shape[0], dtype=jnp.int32)
    seq_weight = jnp.sum(jnp.where(group_ids == seq_group[0], group_weight, 0.0))
    grad_out = permuted(out_grad[0]).astype(f32) * seq_weight
    grad_out_seq = gathered(grad_out.astype(bf16))
    grad_hidden = mm(grad_out_seq, down_all)
    grad_gate = grad_hidden * up_pre * sigmoid_gate * (1.0 + gate_pre * (1.0 - sigmoid_gate))
    grad_up = grad_hidden * silu_gate
    grad_ff = jnp.concatenate([grad_gate.astype(bf16), grad_up.astype(bf16)], axis=1)
    down_share = own_share(mm_tn(grad_out_seq, hidden))
    ff_share = own_share(mm_tn(hat_two_seq, grad_ff))
    grad_hat_two = scattered(mm_nt(grad_ff, ff_all))
    grad_middle = grad_out + norm_back(grad_hat_two, hat_two, inv_two)

    grad_mid_seq = gathered(grad_middle.astype(bf16))
    grad_heads = mm(grad_mid_seq, out_all).astype(bf16).reshape(seq_len, head_count, head_width)
    row_dot = jnp.sum(grad_heads.astype(f32) * attended, axis=2)
    grad_probs = jnp.einsum("thd,kd->htk", grad_heads, values, preferred_element_type=f32)
    grad_scores = (probs * (grad_probs - row_dot.T[:, :, None])).astype(bf16)
    grad_query = jnp.einsum("htk,kd->thd", grad_scores, keys, preferred_element_type=f32)
    grad_keys = jnp.einsum("htk,thd->kd", grad_scores, queries, preferred_element_type=f32)
    grad_values = jnp.einsum("htk,thd->kd", probs_low, grad_heads, preferred_element_type=f32)
    kv_total = scattered(jnp.concatenate([grad_keys, grad_values], axis=1))
    kv_total = kv_total + kv_grad[0].astype(f32)
    key_back = rotate_back(kv_total[:, :head_width], cos_own, sin_own)
    grad_kv_pre = jnp.concatenate([key_back, kv_total[:, head_width:]], axis=1).astype(bf16)
    query_back = rotate_back(grad_query * score_scale, cos_all[:, None, :], sin_all[:, None, :])
    grad_query_pre = query_back.reshape(seq_len, query_cols).astype(bf16)
    grad_hat_one = scattered(mm_nt(grad_query_pre, query_all)) + mm_nt(grad_kv_pre, kv_all)
    input_grad = unpermuted(grad_middle + norm_back(grad_hat_one, hat_one, inv_one))
    attn_share = own_share(
        jnp.concatenate(
            [
                mm_tn(hat_one_seq, grad_query_pre).astype(bf16),
                mm_tn(hat_one_low, grad_kv_pre).astype(bf16),
                mm_tn(grad_mid_seq, attn_rows).astype(bf16),
            ],
            axis=1,
        )
    )
    query_raw = joined(attn_share[:, :, :query_cols])
    kv_raw = jnp.sum(attn_share[:, :, query_cols : query_cols + kv_width], axis=0)
    out_weight_grad = joined(attn_share[:, :, query_cols + kv_width :])
    gate_raw = joined(ff_share[:, :, :ff_cols])
    up_raw = joined(ff_share[:, :, ff_cols:])

    def row_sum(raw, matrix):
        return jnp.sum(raw * matrix.astype(f32), axis=1)

    return (
        layer_out[None],
        shared[None],
        input_grad[None],
        row_sum(query_raw, query_weight) + row_sum(kv_raw, kv_weight),
        query_raw * gain_one,
        kv_raw * gain_one,
        out_weight_grad,
        row_sum(gate_raw, gate_weight) + row_sum(up_raw, up_weight),
        gate_raw * gain_two,
        up_raw * gain_two,
        joined(down_share),
    )


def solution(mesh):
    rows = P("fsdp", "dp", None)
    gain = P(("dp", "fsdp"))
    matrix = P(("dp", "fsdp"), None)
    return jax.shard_map(
        local,
        mesh=mesh,
        in_specs=(
            rows,
            gain,
            matrix,
            matrix,
            matrix,
            gain,
            matrix,
            matrix,
            matrix,
            P("fsdp"),
            P(),
            rows,
            rows,
        ),
        out_specs=(
            rows,
            rows,
            rows,
            gain,
            matrix,
            matrix,
            matrix,
            gain,
            matrix,
            matrix,
            matrix,
        ),
        check_vma=False,
    )
```

time: 3320 us -> 602 us (0.18)
  waiting for transfers between devices: 2880 us -> 317 us
  matrix products: 193 us -> 96.3 us
  other arithmetic: 102 us -> 40.2 us
  starting transfers between devices: 0.68 us -> 48.3 us
  blocking collectives: 91.1 us -> 47 us
    unnamed x12 -> x6, waiting for transfers between devices: 1840 us -> 0.1 us
    all_gather x6 -> x3, waiting for transfers between devices: 535 us -> 85 us  [all_rows(): lax.all_gather(packed.reshape(dp_size * own_rows, packed.shape[2]), 'fsdp...]
    reduce_scatter x4 -> x3, waiting for transfers between devices: 511 us -> 110 us  [own_share(): lax.psum_scatter(grads.astype(bf16), 'fsdp', scatter_dimension=0, tiled=T...]
    ppermute x0 -> x30, waiting for transfers between devices: none -> 110 us  [the longest x15 71.3 us: scattered(): total = total + lax.ppermute(part, 'dp', peers(k)).astype(f32)]
    dot_general x25 -> x20, matrix products: 193 us -> 92.8 us  [the longest x5 32.1 us: mm_nt(): lax.dot_general(left, right, (((1,), (1,)), ((), ())), preferred_element_...]
    concatenate x4 -> x7, other arithmetic: 90.2 us -> 7.37 us  [the longest x1 2.77 us: local(): jnp.concatenate([mm_tn(hat_one_seq, grad_query_pre).astype(bf16), mm_tn(h...]
    unnamed x2 -> x0, blocking collectives: 82.2 us -> none
    all_to_all x0 -> x3, blocking collectives: none -> 47 us  [exchanged(): return lax.all_to_all(packed, 'dp', 0, 0)]
  transfers between devices with their start and end apart: 11 -> 39, of which waited for: 10 -> 22; matrix products, arithmetic and copies ran while one was open for 7% -> 23% of each run, Pallas kernels for 0% -> 0%
where the time goes in v1:
time: 602 us; the launch traced here: 597 us
  waiting for transfers between devices  317 us (53%)
  matrix products  96.3 us (16%)
  starting transfers between devices  48.3 us (8%)
  blocking collectives  47 us (8%)
  other arithmetic  40.2 us (7%)
  local copies, waits for them, and re-layouts  31.8 us (5%)
  between operations  16 us (3%)
    reduce_scatter x3, waiting for transfers between devices, own_share(): lax.psum_scatter(grads.astype(bf16), 'fsdp', scatter_dimension=0, tiled=T...  110 us
    all_gather x3, waiting for transfers between devices, all_rows(): lax.all_gather(packed.reshape(dp_size * own_rows, packed.shape[2]), 'fsdp...  85 us
    ppermute x15, waiting for transfers between devices, scattered(): total = total + lax.ppermute(part, 'dp', peers(k)).astype(f32)  71.3 us
    all_to_all x3, blocking collectives, exchanged(): return lax.all_to_all(packed, 'dp', 0, 0)  47 us
    ppermute x15, waiting for transfers between devices, gathered(): lax.ppermute(block, 'dp', peers(k))  38.5 us
    dot_general x5, matrix products, mm_nt(): lax.dot_general(left, right, (((1,), (1,)), ((), ())), preferred_element_...  32.1 us
    dot_general x5, matrix products, mm(): return jnp.dot(left, right, preferred_element_type=f32)  31.4 us
    dot_general x5, matrix products, mm_tn(): lax.dot_general(left, right, (((0,), (0,)), ((), ())), preferred_element_...  22.5 us
  transfers between devices with their start and end apart: 39, of which 22 were waited for; matrix products, arithmetic and copies ran while one was open for 23% of the time, Pallas kernels for 0%

profile of v1, /device:TPU:0, one launch (start us, length us, event | category | flops | bytes accessed | tf_op | source)
XLA Modules:
  0.0 596.8 jit_solution(17366750395593409068)
XLA Ops:
  11.7 15.0 %all_to_all.30 = bf16[4,64,1280]{2,1,0:T(8,128)(2,1)} all-to-all(bf16[4,64,1280]{2,1,0:T(8,128)(2,1)S(1)} %copy.116), channel_id=1, replica_groups=mesh['dp'=4,'fsdp'=8] {'dp'}, dimensions={0} | all-to-all | bytes 1310720 | tf_op jit(solution)/shard_map/all_to_all | solution.py:109
  28.3 20.5 %all_to_all.31 = bf16[4,64,2816]{2,1,0:T(8,128)(2,1)} all-to-all(bf16[4,64,2816]{2,1,0:T(8,128)(2,1)S(1)} %copy.122), channel_id=1, replica_groups=mesh['dp'=4,'fsdp'=8] {'dp'}, dimensions={0} | all-to-all | bytes 2883584 | tf_op jit(solution)/shard_map/all_to_all | solution.py:109
  49.1 11.5 %all_to_all.32 = bf16[4,64,1408]{2,1,0:T(8,128)(2,1)} all-to-all(bf16[4,64,1408]{2,1,0:T(8,128)(2,1)S(1)} %copy.123), channel_id=1, replica_groups=mesh['dp'=4,'fsdp'=8] {'dp'}, dimensions={0} | all-to-all | bytes 1441792 | tf_op jit(solution)/shard_map/all_to_all | solution.py:109
  68.4 14.2 %all-gather.4.cloned.1.call-done = bf16[2048,1280]{1,0:T(8,128)(2,1)} async-done(((bf16[256,1280]{1,0:T(8,128)(2,1)}), bf16[2048,1280]{1,0:T(8,128)(2,1)}) %all-gather.4.cloned.1.call-update) | async-done | bytes 5242896 | tf_op jit(solution)/shard_map/all_gather | solution.py:112
  105.3 5.1 fusion.84
  118.3 8.3 %collective-permute-done.6 = bf16[128,2048]{1,0:T(8,128)(2,1)} collective-permute-done((bf16[128,2048]{1,0:T(8,128)(2,1)}, bf16[128,2048]{1,0:T(8,128)(2,1)}, u32[]{:S(2)}, u32[]{:S(2)}) %collective-permute-start.6) | collective-permute-done | bytes 524320 | tf_op jit(solution)/shard_map/ppermute | solution.py:101
  126.6 10.4 %collective-permute-done.8 = bf16[128,2048]{1,0:T(8,128)(2,1)} collective-permute-done((bf16[128,2048]{1,0:T(8,128)(2,1)}, bf16[128,2048]{1,0:T(8,128)(2,1)}, u32[]{:S(2)}, u32[]{:S(2)}) %collective-permute-start.8) | collective-permute-done | bytes 524320 | tf_op jit(solution)/shard_map/ppermute | solution.py:101
  149.1 7.5 %collective-permute-done.11 = bf16[128,2048]{1,0:T(8,128)(2,1)S(1)} collective-permute-done((bf16[128,2048]{1,0:T(8,128)(2,1)S(1)}, bf16[128,2048]{1,0:T(8,128)(2,1)S(1)}, u32[]{:S(2)}, u32[]{:S(2)}) %collective-permute-start.11) | collective-permute-done | bytes 524320 | tf_op jit(solution)/shard_map/ppermute | solution.py:93
  158.0 9.8 %collective-permute-done.10 = bf16[128,2048]{1,0:T(8,128)(2,1)S(1)} collective-permute-done((bf16[128,2048]{1,0:T(8,128)(2,1)S(1)}, bf16[128,2048]{1,0:T(8,128)(2,1)S(1)}, u32[]{:S(2)}, u32[]{:S(2)}) %collective-permute-start.10) | collective-permute-done | bytes 524320 | tf_op jit(solution)/shard_map/ppermute | solution.py:93
  168.7 22.4 %all-gather.6.cloned.1.call-done = bf16[2048,2816]{1,0:T(8,128)(2,1)} async-done(((bf16[256,2816]{1,0:T(8,128)(2,1)}), bf16[2048,2816]{1,0:T(8,128)(2,1)}) %all-gather.6.cloned.1.call-update) | async-done | bytes 11534352 | tf_op jit(solution)/shard_map/all_gather | solution.py:112
  191.1 11.8 %fusion.50 = f32[512,2816]{1,0:T(8,128)} fusion(bf16[2048,2816]{1,0:T(8,128)(2,1)} %all-gather.6.cloned.1.call-done, bf16[128,2048]{1,0:T(8,128)(2,1)} %copy-done.46, bf16[128,2048]{1,0:T(8,128)(2,1)} %copy-done.48, bf16[128,2048]{1,0:T(8,128)(2,1)} %collective-permute-done.9, bf16[128,2048]{1,0:T(8,128)(2,1)} %copy-done.33), kind=kOutput, calls=%fused_computation.109 | convolution fusion | flops 5913968640 | bytes 19398656 | tf_op jit(solution)/shard_map/dot_general | solution.py:43
  202.9 48.4 %all-gather.8.cloned.1.call-done = bf16[2048,1408]{1,0:T(8,128)(2,1)} async-done(((bf16[256,1408]{1,0:T(8,128)(2,1)}), bf16[2048,1408]{1,0:T(8,128)(2,1)}) %all-gather.8.cloned.1.call-update) | async-done | bytes 5767184 | tf_op jit(solution)/shard_map/all_gather | solution.py:112
  251.4 11.2 %multiply_convert_fusion.1 = (bf16[512,1408]{1,0:T(8,128)(2,1)}, bf16[512,1408]{1,0:T(8,128)(2,1)}, bf16[512,1408]{1,0:T(8,128)(2,1)S(1)}) fusion(f32[512,2816]{1,0:T(8,128)} %fusion.50, bf16[2048,1408]{1,0:T(8,128)(2,1)} %all-gather.8.cloned.1.call-done, bf16[128,2048]{0,1:T(8,128)(2,1)} %collective-permute-done.17, ...), kind=kOutput, calls=%fused_computation.14 | convolution fusion | flops 2971992064 | bytes 17956864 | tf_op jit(solution)/shard_map/dot_general | solution.py:43
  263.7 7.4 %convolution_convert_fusion.1 = bf16[2048,1408]{1,0:T(8,128)(2,1)} fusion(bf16[512,1408]{1,0:T(8,128)(2,1)S(1)} %get-tuple-element.50, bf16[128,2048]{0,1:T(8,128)(2,1)} %collective-permute-done.17, bf16[128,2048]{0,1:T(8,128)(2,1)} %collective-permute-done.16, bf16[128,2048]{0,1:T(8,128)(2,1)} %collective-permute-done.15, ...), kind=kOutput, calls=%fused_computation.2 | convolution fusion | flops 2964062208 | bytes 9306112 | tf_op jit(solution)/shard_map/dot_general | solution.py:51
  271.2 11.2 %fusion.85 = (bf16[512,2048]{1,0:T(8,128)(2,1)S(1)}, f32[512,2048]{1,0:T(8,128)}) fusion(bf16[2048,2816]{1,0:T(8,128)(2,1)} %all-gather.6.cloned.1.call-done, bf16[512,1408]{1,0:T(8,128)(2,1)} %get-tuple-element.49, bf16[512,1408]{1,0:T(8,128)(2,1)} %get-tuple-element.48), kind=kOutput, calls=%fused_computation.172 | convolution fusion | flops 5912395776 | bytes 20709376 | tf_op jit(solution)/shard_map/dot_general | solution.py:47
  287.0 8.2 %fusion.86 = (bf16[512,2048]{1,0:T(8,128)(2,1)S(1)}, f32[512,2048]{1,0:T(8,128)}) fusion(bf16[512,1408]{1,0:T(8,128)(2,1)S(1)} %copy-done.59, bf16[2048,1408]{1,0:T(8,128)(2,1)} %all-gather.8.cloned.1.call-done), kind=kOutput, calls=%fused_computation.173 | convolution fusion | flops 2953838592 | bytes 13500416 | tf_op jit(solution)/shard_map/dot_general | solution.py:47
  302.4 8.2 %collective-permute-done.20 = bf16[128,2048]{1,0:T(8,128)(2,1)} collective-permute-done((bf16[128,2048]{1,0:T(8,128)(2,1)}, bf16[128,2048]{1,0:T(8,128)(2,1)}, u32[]{:S(2)}, u32[]{:S(2)}) %collective-permute-start.20) | collective-permute-done | bytes 524320 | tf_op jit(solution)/shard_map/ppermute | solution.py:101
  315.2 5.7 collective-permute-done.12
  320.9 11.5 %collective-permute-done.14 = bf16[128,2048]{1,0:T(8,128)(2,1)} collective-permute-done((bf16[128,2048]{1,0:T(8,128)(2,1)}, bf16[128,2048]{1,0:T(8,128)(2,1)}, u32[]{:S(2)}, u32[]{:S(2)}) %collective-permute-start.14) | collective-permute-done | bytes 524320 | tf_op jit(solution)/shard_map/ppermute | solution.py:101
  333.9 4.7 fusion.74
  342.1 12.2 %collective-permute-done.23 = bf16[128,2048]{1,0:T(8,128)(2,1)S(1)} collective-permute-done((bf16[128,2048]{1,0:T(8,128)(2,1)S(1)}, bf16[128,2048]{1,0:T(8,128)(2,1)S(1)}, u32[]{:S(2)}, u32[]{:S(2)}) %collective-permute-start.23) | collective-permute-done | bytes 524320 | tf_op jit(solution)/shard_map/ppermute | solution.py:93
  354.3 9.0 %collective-permute-done.22 = bf16[128,2048]{1,0:T(8,128)(2,1)S(1)} collective-permute-done((bf16[128,2048]{1,0:T(8,128)(2,1)S(1)}, bf16[128,2048]{1,0:T(8,128)(2,1)S(1)}, u32[]{:S(2)}, u32[]{:S(2)}) %collective-permute-start.22) | collective-permute-done | bytes 524320 | tf_op jit(solution)/shard_map/ppermute | solution.py:93
  389.1 11.0 %convolution_convert_fusion = bf16[2048,2816]{1,0:T(8,128)(2,1)} fusion(bf16[512,1408]{1,0:T(8,128)(2,1)} %get-tuple-element.49, bf16[512,1408]{1,0:T(8,128)(2,1)} %get-tuple-element.48, bf16[128,2048]{1,0:T(8,128)(2,1)S(1)} %copy-done.47, bf16[128,2048]{1,0:T(8,128)(2,1)S(1)} %copy-done.49, bf16[128,2048]{1,0:T(8,128)(2,1)} %collective-permute-done.9, ...), kind=kOutput, calls=%fused_computation.1 | convolution fusion | flops 5925502976 | bytes 16515072 | tf_op jit(solution)/shard_map/dot_general | solution.py:51
  400.1 4.9 fusion.87
  412.6 4.2 all-to-all-start.5
  416.7 4.4 collective-permute-done.24
  421.2 11.8 %collective-permute-done.26 = bf16[128,2048]{1,0:T(8,128)(2,1)S(1)} collective-permute-done((bf16[128,2048]{1,0:T(8,128)(2,1)}, bf16[128,2048]{1,0:T(8,128)(2,1)S(1)}, u32[]{:S(2)}, u32[]{:S(2)}) %collective-permute-start.26) | collective-permute-done | bytes 524320 | tf_op jit(solution)/shard_map/ppermute | solution.py:101
  432.9 5.9 collective-permute-done.25
  441.7 4.0 reduce-scatter.4.cloned.1.call-done
  447.8 4.2 all-to-all-start.3
  459.9 105.6 %reduce-scatter.6.cloned.1.call-done = bf16[256,2816]{1,0:T(8,128)(2,1)} async-done(((bf16[2048,2816]{1,0:T(8,128)(2,1)}), bf16[256,2816]{1,0:T(8,128)(2,1)}) %reduce-scatter.6.cloned.1.call-update) | async-done | bytes 1441808 | tf_op jit(solution)/shard_map/reduce_scatter | solution.py:117
  576.3 9.0 %all-to-all-done.4 = bf16[4,64,2816]{2,1,0:T(8,128)(2,1)S(1)} async-done(((bf16[4,64,2816]{2,1,0:T(8,128)(2,1)}), bf16[4,64,2816]{2,1,0:T(8,128)(2,1)S(1)}, u32[]{:S(2)}, u32[]{:S(2)}) %all-to-all-start.4) | async-done | bytes 1441824 | tf_op jit(solution)/shard_map/all_to_all | solution.py:109
  (287 shorter events, 141.8 us)
Async XLA Ops:
  7.2 75.4 %all-gather.4.cloned.1.call-start = ((), (), s32[]{:S(2)}) async-start(), calls=%async_computation.9 | async-start | bytes 5898240 | tf_op jit(solution)/shard_map/all_gather | solution.py:112
  26.7 164.3 %all-gather.6.cloned.1.call-start = ((), (), s32[]{:S(2)}) async-start(), calls=%async_computation.10 | async-start | bytes 12976128 | tf_op jit(solution)/shard_map/all_gather | solution.py:112
  48.8 202.6 %all-gather.8.cloned.1.call-start = ((), (), s32[]{:S(2)}) async-start(), calls=%async_computation.11 | async-start | bytes 6488064 | tf_op jit(solution)/shard_map/all_gather | solution.py:112
  60.7 351.9 %reduce-scatter.8.cloned.1.call-start = ((), (), s32[]{:S(2)}) async-start(), calls=%async_computation.14 | async-start | bytes 6488064 | tf_op jit(solution)/shard_map/reduce_scatter | solution.py:117
  61.9 25.9 %collective-permute-start.5 = (bf16[128,2048]{1,0:T(8,128)(2,1)S(1)}, bf16[128,2048]{1,0:T(8,128)(2,1)S(1)}, u32[]{:S(2)}, u32[]{:S(2)}) collective-permute-start(bf16[128,2048]{1,0:T(8,128)(2,1)S(1)} %multiply_convert_fusion.4), channel_id=1, source_target_pairs={{0,24},{8,16},{16,8},{24,0},{1,25},{9,17},{17,9},{25,1},{2,26},{10... | collective-permute-start | bytes 1572872 | tf_op jit(solution)/shard_map/ppermute | solution.py:93
  62.8 25.7 %collective-permute-start.4 = (bf16[128,2048]{1,0:T(8,128)(2,1)S(1)}, bf16[128,2048]{1,0:T(8,128)(2,1)S(1)}, u32[]{:S(2)}, u32[]{:S(2)}) collective-permute-start(bf16[128,2048]{1,0:T(8,128)(2,1)S(1)} %multiply_convert_fusion.4), channel_id=1, source_target_pairs={{0,16},{8,24},{16,0},{24,8},{1,17},{9,25},{17,1},{25,9},{2,18},{10... | collective-permute-start | bytes 1572872 | tf_op jit(solution)/shard_map/ppermute | solution.py:93
  64.2 24.2 %collective-permute-start.3 = (bf16[128,2048]{1,0:T(8,128)(2,1)S(1)}, bf16[128,2048]{1,0:T(8,128)(2,1)}, u32[]{:S(2)}, u32[]{:S(2)}) collective-permute-start(bf16[128,2048]{1,0:T(8,128)(2,1)S(1)} %multiply_convert_fusion.4), channel_id=1, source_target_pairs={{0,8},{8,0},{16,24},{24,16},{1,9},{9,1},{17,25},{25,17},{2,10},{10... | collective-permute-start | bytes 1572872 | tf_op jit(solution)/shard_map/ppermute | solution.py:93
  111.5 15.1 %collective-permute-start.6 = (bf16[128,2048]{1,0:T(8,128)(2,1)}, bf16[128,2048]{1,0:T(8,128)(2,1)}, u32[]{:S(2)}, u32[]{:S(2)}) collective-permute-start(bf16[128,2048]{1,0:T(8,128)(2,1)} %get-tuple-element.64), channel_id=1, source_target_pairs={{0,8},{8,0},{16,24},{24,16},{1,9},{9,1},{17,25},{25,17},{2,10},{10... | collective-permute-start | bytes 1572872 | tf_op jit(solution)/shard_map/ppermute | solution.py:101
  113.1 24.0 %collective-permute-start.8 = (bf16[128,2048]{1,0:T(8,128)(2,1)}, bf16[128,2048]{1,0:T(8,128)(2,1)}, u32[]{:S(2)}, u32[]{:S(2)}) collective-permute-start(bf16[128,2048]{1,0:T(8,128)(2,1)} %get-tuple-element.65), channel_id=1, source_target_pairs={{0,24},{8,16},{16,8},{24,0},{1,25},{9,17},{17,9},{25,1},{2,26},{10... | collective-permute-start | bytes 1572872 | tf_op jit(solution)/shard_map/ppermute | solution.py:101
  114.5 23.9 %collective-permute-start.7 = (bf16[128,2048]{1,0:T(8,128)(2,1)}, bf16[128,2048]{1,0:T(8,128)(2,1)}, u32[]{:S(2)}, u32[]{:S(2)}) collective-permute-start(bf16[128,2048]{1,0:T(8,128)(2,1)} %get-tuple-element.66), channel_id=1, source_target_pairs={{0,16},{8,24},{16,0},{24,8},{1,17},{9,25},{17,1},{25,9},{2,18},{10... | collective-permute-start | bytes 1572872 | tf_op jit(solution)/shard_map/ppermute | solution.py:101
  140.8 15.8 %collective-permute-start.11 = (bf16[128,2048]{1,0:T(8,128)(2,1)S(1)}, bf16[128,2048]{1,0:T(8,128)(2,1)S(1)}, u32[]{:S(2)}, u32[]{:S(2)}) collective-permute-start(bf16[128,2048]{1,0:T(8,128)(2,1)S(1)} %multiply_convert_fusion.3), channel_id=1, source_target_pairs={{0,24},{8,16},{16,8},{24,0},{1,25},{9,17},{17,9},{25,1},{2,26},{10... | collective-permute-start | bytes 1572872 | tf_op jit(solution)/shard_map/ppermute | solution.py:93
  142.4 25.5 %collective-permute-start.10 = (bf16[128,2048]{1,0:T(8,128)(2,1)S(1)}, bf16[128,2048]{1,0:T(8,128)(2,1)S(1)}, u32[]{:S(2)}, u32[]{:S(2)}) collective-permute-start(bf16[128,2048]{1,0:T(8,128)(2,1)S(1)} %multiply_convert_fusion.3), channel_id=1, source_target_pairs={{0,16},{8,24},{16,0},{24,8},{1,17},{9,25},{17,1},{25,9},{2,18},{10... | collective-permute-start | bytes 1572872 | tf_op jit(solution)/shard_map/ppermute | solution.py:93
  143.8 24.9 %collective-permute-start.9 = (bf16[128,2048]{1,0:T(8,128)(2,1)S(1)}, bf16[128,2048]{1,0:T(8,128)(2,1)}, u32[]{:S(2)}, u32[]{:S(2)}) collective-permute-start(bf16[128,2048]{1,0:T(8,128)(2,1)S(1)} %multiply_convert_fusion.3), channel_id=1, source_target_pairs={{0,8},{8,0},{16,24},{24,16},{1,9},{9,1},{17,25},{25,17},{2,10},{10... | collective-permute-start | bytes 1572872 | tf_op jit(solution)/shard_map/ppermute | solution.py:93
  146.2 56.7 %collective-permute-start.17 = (bf16[128,2048]{0,1:T(8,128)(2,1)}, bf16[128,2048]{0,1:T(8,128)(2,1)}, u32[]{:S(2)}, u32[]{:S(2)}) collective-permute-start(bf16[128,2048]{0,1:T(8,128)(2,1)} %bitcast_convert_fusion), channel_id=1, source_target_pairs={{0,24},{8,16},{16,8},{24,0},{1,25},{9,17},{17,9},{25,1},{2,26},{10... | collective-permute-start | bytes 1572872 | tf_op jit(solution)/shard_map/ppermute | solution.py:93
  147.7 55.2 %collective-permute-start.16 = (bf16[128,2048]{0,1:T(8,128)(2,1)}, bf16[128,2048]{0,1:T(8,128)(2,1)}, u32[]{:S(2)}, u32[]{:S(2)}) collective-permute-start(bf16[128,2048]{0,1:T(8,128)(2,1)} %bitcast_convert_fusion), channel_id=1, source_target_pairs={{0,16},{8,24},{16,0},{24,8},{1,17},{9,25},{17,1},{25,9},{2,18},{10... | collective-permute-start | bytes 1572872 | tf_op jit(solution)/shard_map/ppermute | solution.py:93
  156.6 46.3 %collective-permute-start.15 = (bf16[128,2048]{0,1:T(8,128)(2,1)}, bf16[128,2048]{0,1:T(8,128)(2,1)}, u32[]{:S(2)}, u32[]{:S(2)}) collective-permute-start(bf16[128,2048]{0,1:T(8,128)(2,1)} %bitcast_convert_fusion), channel_id=1, source_target_pairs={{0,8},{8,0},{16,24},{24,16},{1,9},{9,1},{17,25},{25,17},{2,10},{10... | collective-permute-start | bytes 1572872 | tf_op jit(solution)/shard_map/ppermute | solution.py:93
  271.1 174.5 %reduce-scatter.4.cloned.1.call-start = ((), (), s32[]{:S(2)}) async-start(), calls=%async_computation.12 | async-start | bytes 5898240 | tf_op jit(solution)/shard_map/reduce_scatter | solution.py:117
  283.5 15.8 %collective-permute-start.18 = (bf16[128,2048]{1,0:T(8,128)(2,1)S(1)}, bf16[128,2048]{1,0:T(8,128)(2,1)}, u32[]{:S(2)}, u32[]{:S(2)}) collective-permute-start(bf16[128,2048]{1,0:T(8,128)(2,1)S(1)} %get-tuple-element.58), channel_id=1, source_target_pairs={{0,8},{8,0},{16,24},{24,16},{1,9},{9,1},{17,25},{25,17},{2,10},{10... | collective-permute-start | bytes 1572872 | tf_op jit(solution)/shard_map/ppermute | solution.py:101
  284.9 25.6 %collective-permute-start.20 = (bf16[128,2048]{1,0:T(8,128)(2,1)}, bf16[128,2048]{1,0:T(8,128)(2,1)}, u32[]{:S(2)}, u32[]{:S(2)}) collective-permute-start(bf16[128,2048]{1,0:T(8,128)(2,1)} %get-tuple-element.59), channel_id=1, source_target_pairs={{0,24},{8,16},{16,8},{24,0},{1,25},{9,17},{17,9},{25,1},{2,26},{10... | collective-permute-start | bytes 1572872 | tf_op jit(solution)/shard_map/ppermute | solution.py:101
  286.4 26.3 %collective-permute-start.19 = (bf16[128,2048]{1,0:T(8,128)(2,1)}, bf16[128,2048]{1,0:T(8,128)(2,1)}, u32[]{:S(2)}, u32[]{:S(2)}) collective-permute-start(bf16[128,2048]{1,0:T(8,128)(2,1)} %get-tuple-element.60), channel_id=1, source_target_pairs={{0,16},{8,24},{16,0},{24,8},{1,17},{9,25},{17,1},{25,9},{2,18},{10... | collective-permute-start | bytes 1572872 | tf_op jit(solution)/shard_map/ppermute | solution.py:101
  296.4 24.5 %collective-permute-start.12 = (bf16[128,2048]{1,0:T(8,128)(2,1)}, bf16[128,2048]{1,0:T(8,128)(2,1)}, u32[]{:S(2)}, u32[]{:S(2)}) collective-permute-start(bf16[128,2048]{1,0:T(8,128)(2,1)} %get-tuple-element.61), channel_id=1, source_target_pairs={{0,8},{8,0},{16,24},{24,16},{1,9},{9,1},{17,25},{25,17},{2,10},{10... | collective-permute-start | bytes 1572872 | tf_op jit(solution)/shard_map/ppermute | solution.py:101
  297.8 34.6 %collective-permute-start.14 = (bf16[128,2048]{1,0:T(8,128)(2,1)}, bf16[128,2048]{1,0:T(8,128)(2,1)}, u32[]{:S(2)}, u32[]{:S(2)}) collective-permute-start(bf16[128,2048]{1,0:T(8,128)(2,1)} %get-tuple-element.62), channel_id=1, source_target_pairs={{0,24},{8,16},{16,8},{24,0},{1,25},{9,17},{17,9},{25,1},{2,26},{10... | collective-permute-start | bytes 1572872 | tf_op jit(solution)/shard_map/ppermute | solution.py:101
  299.3 34.6 %collective-permute-start.13 = (bf16[128,2048]{1,0:T(8,128)(2,1)}, bf16[128,2048]{1,0:T(8,128)(2,1)}, u32[]{:S(2)}, u32[]{:S(2)}) collective-permute-start(bf16[128,2048]{1,0:T(8,128)(2,1)} %get-tuple-element.63), channel_id=1, source_target_pairs={{0,16},{8,24},{16,0},{24,8},{1,17},{9,25},{17,1},{25,9},{2,18},{10... | collective-permute-start | bytes 1572872 | tf_op jit(solution)/shard_map/ppermute | solution.py:101
  338.6 15.7 %collective-permute-start.23 = (bf16[128,2048]{1,0:T(8,128)(2,1)S(1)}, bf16[128,2048]{1,0:T(8,128)(2,1)S(1)}, u32[]{:S(2)}, u32[]{:S(2)}) collective-permute-start(bf16[128,2048]{1,0:T(8,128)(2,1)S(1)} %get-tuple-element.44), channel_id=1, source_target_pairs={{0,24},{8,16},{16,8},{24,0},{1,25},{9,17},{17,9},{25,1},{2,26},{10... | collective-permute-start | bytes 1572872 | tf_op jit(solution)/shard_map/ppermute | solution.py:93
  340.1 23.3 %collective-permute-start.22 = (bf16[128,2048]{1,0:T(8,128)(2,1)S(1)}, bf16[128,2048]{1,0:T(8,128)(2,1)S(1)}, u32[]{:S(2)}, u32[]{:S(2)}) collective-permute-start(bf16[128,2048]{1,0:T(8,128)(2,1)S(1)} %get-tuple-element.44), channel_id=1, source_target_pairs={{0,16},{8,24},{16,0},{24,8},{1,17},{9,25},{17,1},{25,9},{2,18},{10... | collective-permute-start | bytes 1572872 | tf_op jit(solution)/shard_map/ppermute | solution.py:93
  341.6 21.8 %collective-permute-start.21 = (bf16[128,2048]{1,0:T(8,128)(2,1)S(1)}, bf16[128,2048]{1,0:T(8,128)(2,1)S(1)}, u32[]{:S(2)}, u32[]{:S(2)}) collective-permute-start(bf16[128,2048]{1,0:T(8,128)(2,1)S(1)} %get-tuple-element.44), channel_id=1, source_target_pairs={{0,8},{8,0},{16,24},{24,16},{1,9},{9,1},{17,25},{25,17},{2,10},{10... | collective-permute-start | bytes 1572872 | tf_op jit(solution)/shard_map/ppermute | solution.py:93
  387.8 177.7 %reduce-scatter.6.cloned.1.call-start = ((), (), s32[]{:S(2)}) async-start(), calls=%async_computation.13 | async-start | bytes 12976128 | tf_op jit(solution)/shard_map/reduce_scatter | solution.py:117
  406.2 15.0 %collective-permute-start.24 = (bf16[128,2048]{1,0:T(8,128)(2,1)}, bf16[128,2048]{1,0:T(8,128)(2,1)S(1)}, u32[]{:S(2)}, u32[]{:S(2)}) collective-permute-start(bf16[128,2048]{1,0:T(8,128)(2,1)} %get-tuple-element.55), channel_id=1, source_target_pairs={{0,8},{8,0},{16,24},{24,16},{1,9},{9,1},{17,25},{25,17},{2,10},{10... | collective-permute-start | bytes 1572872 | tf_op jit(solution)/shard_map/ppermute | solution.py:101
  407.2 25.8 %collective-permute-start.26 = (bf16[128,2048]{1,0:T(8,128)(2,1)}, bf16[128,2048]{1,0:T(8,128)(2,1)S(1)}, u32[]{:S(2)}, u32[]{:S(2)}) collective-permute-start(bf16[128,2048]{1,0:T(8,128)(2,1)} %get-tuple-element.56), channel_id=1, source_target_pairs={{0,24},{8,16},{16,8},{24,0},{1,25},{9,17},{17,9},{25,1},{2,26},{10... | collective-permute-start | bytes 1572872 | tf_op jit(solution)/shard_map/ppermute | solution.py:101
  408.6 30.2 %collective-permute-start.25 = (bf16[128,2048]{1,0:T(8,128)(2,1)}, bf16[128,2048]{1,0:T(8,128)(2,1)}, u32[]{:S(2)}, u32[]{:S(2)}) collective-permute-start(bf16[128,2048]{1,0:T(8,128)(2,1)} %get-tuple-element.57), channel_id=1, source_target_pairs={{0,16},{8,24},{16,0},{24,8},{1,17},{9,25},{17,1},{25,9},{2,18},{10... | collective-permute-start | bytes 1572872 | tf_op jit(solution)/shard_map/ppermute | solution.py:101
  412.6 35.2 %all-to-all-start.5 = ((bf16[4,64,1408]{2,1,0:T(8,128)(2,1)}), bf16[4,64,1408]{2,1,0:T(8,128)(2,1)}, u32[]{:S(2)}, u32[]{:S(2)}) async-start(bf16[4,64,1408]{2,1,0:T(8,128)(2,1)} %bitcast.157), calls=%async_computation.8 | async-start | bytes 1441792 | tf_op jit(solution)/shard_map/all_to_all | solution.py:109
  565.5 19.8 %all-to-all-start.4 = ((bf16[4,64,2816]{2,1,0:T(8,128)(2,1)}), bf16[4,64,2816]{2,1,0:T(8,128)(2,1)S(1)}, u32[]{:S(2)}, u32[]{:S(2)}) async-start(bf16[4,64,2816]{2,1,0:T(8,128)(2,1)} %bitcast.152), calls=%async_computation.6 | async-start | bytes 2883584 | tf_op jit(solution)/shard_map/all_to_all | solution.py:109
  (67 other events, 568.7 us)
Sparse Core Ops, SparseCore 0:
  26.8 55.6 all-gather.3
  84.2 106.8 all-gather.5
  192.7 58.6 all-gather.7
  271.2 63.4 reduce-scatter.7
  387.9 57.6 reduce-scatter.3
  447.8 117.6 reduce-scatter.5

commit v2 on v1

--- a/solution.py
+++ b/solution.py
@@ -113,9 +113,11 @@
             packed.reshape(dp_size * own_rows, packed.shape[2]), "fsdp", axis=0, tiled=True
         )
 
-    def own_share(grads):
-        share = lax.psum_scatter(grads.astype(bf16), "fsdp", scatter_dimension=0, tiled=True)
-        return exchanged(share.reshape(dp_size, own_rows, grads.shape[1])).astype(f32)
+    def summed(grads):
+        return lax.psum_scatter(grads.astype(bf16), "fsdp", scatter_dimension=0, tiled=True)
+
+    def own_share(share):
+        return exchanged(share.reshape(dp_size, own_rows, share.shape[1])).astype(f32)
 
     def joined(blocks):
         return blocks.transpose(1, 0, 2).reshape(own_rows, dp_size * blocks.shape[2])
@@ -186,22 +188,29 @@
     sigmoid_gate = jax.nn.sigmoid(gate_pre)
     silu_gate = gate_pre * sigmoid_gate
     hidden = (silu_gate * up_pre).astype(bf16)
-    layer_out = unpermuted((middle + scattered(mm_nt(hidden, down_all))).astype(bf16))
 
     group_ids = jnp.arange(group_weight.shape[0], dtype=jnp.int32)
     seq_weight = jnp.sum(jnp.where(group_ids == seq_group[0], group_weight, 0.0))
     grad_out = permuted(out_grad[0]).astype(f32) * seq_weight
     grad_out_seq = gathered(grad_out.astype(bf16))
+    down_grad = mm_tn(grad_out_seq, hidden).astype(bf16)
+    down_all, down_grad = lax.optimization_barrier((down_all, down_grad))
+    down_sum = summed(down_grad)
     grad_hidden = mm(grad_out_seq, down_all)
     grad_gate = grad_hidden * up_pre * sigmoid_gate * (1.0 + gate_pre * (1.0 - sigmoid_gate))
     grad_up = grad_hidden * silu_gate
     grad_ff = jnp.concatenate([grad_gate.astype(bf16), grad_up.astype(bf16)], axis=1)
-    down_share = own_share(mm_tn(grad_out_seq, hidden))
-    ff_share = own_share(mm_tn(hat_two_seq, grad_ff))
     grad_hat_two = scattered(mm_nt(grad_ff, ff_all))
+    ff_grad = mm_tn(hat_two_seq, grad_ff).astype(bf16)
+    grad_hat_two, ff_grad = lax.optimization_barrier((grad_hat_two, ff_grad))
+    ff_grad, down_sum = lax.optimization_barrier((ff_grad, down_sum))
+    ff_sum = summed(ff_grad)
+    down_share = own_share(down_sum)
     grad_middle = grad_out + norm_back(grad_hat_two, hat_two, inv_two)
 
     grad_mid_seq = gathered(grad_middle.astype(bf16))
+    late_hidden, grad_mid_seq = lax.optimization_barrier((hidden, grad_mid_seq))
+    layer_out = unpermuted((middle + scattered(mm_nt(late_hidden, down_all))).astype(bf16))
     grad_heads = mm(grad_mid_seq, out_all).astype(bf16).reshape(seq_len, head_count, head_width)
     row_dot = jnp.sum(grad_heads.astype(f32) * attended, axis=2)
     grad_probs = jnp.einsum("thd,kd->htk", grad_heads, values, preferred_element_type=f32)
@@ -217,16 +226,17 @@
     grad_query_pre = query_back.reshape(seq_len, query_cols).astype(bf16)
     grad_hat_one = scattered(mm_nt(grad_query_pre, query_all)) + mm_nt(grad_kv_pre, kv_all)
     input_grad = unpermuted(grad_middle + norm_back(grad_hat_one, hat_one, inv_one))
-    attn_share = own_share(
-        jnp.concatenate(
-            [
-                mm_tn(hat_one_seq, grad_query_pre).astype(bf16),
-                mm_tn(hat_one_low, grad_kv_pre).astype(bf16),
-                mm_tn(grad_mid_seq, attn_rows).astype(bf16),
-            ],
-            axis=1,
-        )
-    )
+    attn_grad = jnp.concatenate(
+        [
+            mm_tn(hat_one_seq, grad_query_pre).astype(bf16),
+            mm_tn(hat_one_low, grad_kv_pre).astype(bf16),
+            mm_tn(grad_mid_seq, attn_rows).astype(bf16),
+        ],
+        axis=1,
+    )
+    attn_grad, ff_sum = lax.optimization_barrier((attn_grad, ff_sum))
+    ff_share = own_share(ff_sum)
+    attn_share = own_share(summed(attn_grad))
     query_raw = joined(attn_share[:, :, :query_cols])
     kv_raw = jnp.sum(attn_share[:, :, query_cols : query_cols + kv_width], axis=0)
     out_weight_grad = joined(attn_share[:, :, query_cols + kv_width :])

time: 602 us -> 555 us (0.922)
  waiting for transfers between devices: 317 us -> 275 us
  blocking collectives: 47 us -> 35.5 us
    reduce_scatter x3, waiting for transfers between devices: 110 us -> 79.6 us  [summed(): lax.psum_scatter(grads.astype(bf16), 'fsdp', scatter_dimension=0, tiled=T...]
    all_gather x3, waiting for transfers between devices: 85 us -> 69.1 us  [all_rows(): lax.all_gather(packed.reshape(dp_size * own_rows, packed.shape[2]), 'fsdp...]
    all_to_all x3 -> x2, blocking collectives: 47 us -> 35.5 us  [exchanged(): return lax.all_to_all(packed, 'dp', 0, 0)]
    all_to_all x3 -> x4, waiting for transfers between devices: 12.7 us -> 19.2 us  [exchanged(): return lax.all_to_all(packed, 'dp', 0, 0)]
    unnamed x128 -> x112, local copies, waits for them, and re-layouts: 11.4 us -> 16.3 us
    all_to_all x3 -> x4, starting transfers between devices: 12 us -> 14 us  [exchanged(): return lax.all_to_all(packed, 'dp', 0, 0)]
  transfers between devices with their start and end apart: 39 -> 40, of which waited for: 22 -> 26; matrix products, arithmetic and copies ran while one was open for 23% -> 27% of each run, Pallas kernels for 0% -> 0%
where the time goes in v2:
time: 555 us; the launch traced here: 545 us
  waiting for transfers between devices  275 us (50%)
  matrix products  91.8 us (17%)
  starting transfers between devices  51.9 us (9%)
  other arithmetic  39.4 us (7%)
  local copies, waits for them, and re-layouts  35.6 us (6%)
  blocking collectives  35.5 us (6%)
  between operations  16 us (3%)
    reduce_scatter x3, waiting for transfers between devices, summed(): lax.psum_scatter(grads.astype(bf16), 'fsdp', scatter_dimension=0, tiled=T...  79.6 us
    ppermute x15, waiting for transfers between devices, scattered(): total = total + lax.ppermute(part, 'dp', peers(k)).astype(f32)  69.1 us
    all_gather x3, waiting for transfers between devices, all_rows(): lax.all_gather(packed.reshape(dp_size * own_rows, packed.shape[2]), 'fsdp...  69.1 us
    ppermute x15, waiting for transfers between devices, gathered(): lax.ppermute(block, 'dp', peers(k))  37.7 us
    all_to_all x2, blocking collectives, exchanged(): return lax.all_to_all(packed, 'dp', 0, 0)  35.5 us
    dot_general x5, matrix products, mm_nt(): lax.dot_general(left, right, (((1,), (1,)), ((), ())), preferred_element_...  30 us
    dot_general x5, matrix products, mm(): return jnp.dot(left, right, preferred_element_type=f32)  28.2 us
    dot_general x5, matrix products, mm_tn(): lax.dot_general(left, right, (((0,), (0,)), ((), ())), preferred_element_...  22.5 us
  transfers between devices with their start and end apart: 40, of which 26 were waited for; matrix products, arithmetic and copies ran while one was open for 27% of the time, Pallas kernels for 0%

profile of v2, /device:TPU:0, one launch (start us, length us, event | category | flops | bytes accessed | tf_op | source)
XLA Modules:
  0.0 545.0 jit_solution(2815031784034718017)
XLA Ops:
  11.7 15.0 %all_to_all.30 = bf16[4,64,1280]{2,1,0:T(8,128)(2,1)} all-to-all(bf16[4,64,1280]{2,1,0:T(8,128)(2,1)S(1)} %copy.116), channel_id=1, replica_groups=mesh['dp'=4,'fsdp'=8] {'dp'}, dimensions={0} | all-to-all | bytes 1310720 | tf_op jit(solution)/shard_map/all_to_all | solution.py:109
  28.3 20.5 %all_to_all.31 = bf16[4,64,2816]{2,1,0:T(8,128)(2,1)} all-to-all(bf16[4,64,2816]{2,1,0:T(8,128)(2,1)S(1)} %copy.122), channel_id=1, replica_groups=mesh['dp'=4,'fsdp'=8] {'dp'}, dimensions={0} | all-to-all | bytes 2883584 | tf_op jit(solution)/shard_map/all_to_all | solution.py:109
  50.0 3.5 all-to-all-start.2
  58.3 13.0 %all-to-all-done.2 = bf16[4,64,1408]{2,1,0:T(8,128)(2,1)S(1)} async-done(((bf16[4,64,1408]{2,1,0:T(8,128)(2,1)}), bf16[4,64,1408]{2,1,0:T(8,128)(2,1)S(1)}, u32[]{:S(2)}, u32[]{:S(2)}) %all-to-all-start.2) | async-done | bytes 720928 | tf_op jit(solution)/shard_map/all_to_all | solution.py:109
  75.1 7.4 %all-gather.4.cloned.1.call-done = bf16[2048,1280]{1,0:T(8,128)(2,1)} async-done(((bf16[256,1280]{1,0:T(8,128)(2,1)}), bf16[2048,1280]{1,0:T(8,128)(2,1)}) %all-gather.4.cloned.1.call-update) | async-done | bytes 5242896 | tf_op jit(solution)/shard_map/all_gather | solution.py:112
  88.5 3.5 fusion.14
  97.5 3.5 fusion.80
  105.4 5.1 fusion.82
  117.8 8.9 %collective-permute-done.6 = bf16[128,2048]{1,0:T(8,128)(2,1)S(1)} collective-permute-done((bf16[128,2048]{1,0:T(8,128)(2,1)}, bf16[128,2048]{1,0:T(8,128)(2,1)S(1)}, u32[]{:S(2)}, u32[]{:S(2)}) %collective-permute-start.6) | collective-permute-done | bytes 524320 | tf_op jit(solution)/shard_map/ppermute | solution.py:101
  126.8 10.4 %collective-permute-done.8 = bf16[128,2048]{1,0:T(8,128)(2,1)S(1)} collective-permute-done((bf16[128,2048]{1,0:T(8,128)(2,1)}, bf16[128,2048]{1,0:T(8,128)(2,1)S(1)}, u32[]{:S(2)}, u32[]{:S(2)}) %collective-permute-start.8) | collective-permute-done | bytes 524320 | tf_op jit(solution)/shard_map/ppermute | solution.py:101
  149.8 7.3 %collective-permute-done.11 = bf16[128,2048]{1,0:T(8,128)(2,1)S(1)} collective-permute-done((bf16[128,2048]{1,0:T(8,128)(2,1)S(1)}, bf16[128,2048]{1,0:T(8,128)(2,1)S(1)}, u32[]{:S(2)}, u32[]{:S(2)}) %collective-permute-start.11) | collective-permute-done | bytes 524320 | tf_op jit(solution)/shard_map/ppermute | solution.py:93
  158.6 9.8 %collective-permute-done.10 = bf16[128,2048]{1,0:T(8,128)(2,1)S(1)} collective-permute-done((bf16[128,2048]{1,0:T(8,128)(2,1)S(1)}, bf16[128,2048]{1,0:T(8,128)(2,1)S(1)}, u32[]{:S(2)}, u32[]{:S(2)}) %collective-permute-start.10) | collective-permute-done | bytes 524320 | tf_op jit(solution)/shard_map/ppermute | solution.py:93
  169.3 21.8 %all-gather.6.cloned.1.call-done = bf16[2048,2816]{1,0:T(8,128)(2,1)} async-done(((bf16[256,2816]{1,0:T(8,128)(2,1)}), bf16[2048,2816]{1,0:T(8,128)(2,1)}) %all-gather.6.cloned.1.call-update) | async-done | bytes 11534352 | tf_op jit(solution)/shard_map/all_gather | solution.py:112
  191.1 10.1 %fusion.50 = f32[512,2816]{1,0:T(8,128)S(1)} fusion(bf16[2048,2816]{1,0:T(8,128)(2,1)} %all-gather.6.cloned.1.call-done, bf16[128,2048]{1,0:T(8,128)(2,1)} %copy-done.46, bf16[128,2048]{1,0:T(8,128)(2,1)} %copy-done.48, bf16[128,2048]{1,0:T(8,128)(2,1)} %collective-permute-done.9, bf16[128,2048]{1,0:T(8,128)(2,1)S(1)} %multiply_convert_fusion.3), kind=kOutput, calls=%fused_computation.109 | convolution fusion | flops 5913968640 | bytes 19398656 | tf_op jit(solution)/shard_map/dot_general | solution.py:43
  204.8 7.3 %convolution_convert_fusion.1 = bf16[2048,1408]{1,0:T(8,128)(2,1)} fusion(bf16[512,1408]{1,0:T(8,128)(2,1)S(1)} %multiply_convert_fusion.2, bf16[128,2048]{0,1:T(8,128)(2,1)} %collective-permute-done.14, bf16[128,2048]{0,1:T(8,128)(2,1)} %collective-permute-done.13, bf16[128,2048]{0,1:T(8,128)(2,1)} %collective-permute-done.12, ...), kind=kOutput, calls=%fused_computation.2 | convolution fusion | flops 2964062208 | bytes 9306112 | tf_op jit(solution)/shard_map/dot_general | solution.py:51
  212.1 39.9 %all-gather.8.cloned.1.call-done = bf16[2048,1408]{1,0:T(8,128)(2,1)} async-done(((bf16[256,1408]{1,0:T(8,128)(2,1)}), bf16[2048,1408]{1,0:T(8,128)(2,1)}) %all-gather.8.cloned.1.call-update) | async-done | bytes 5767184 | tf_op jit(solution)/shard_map/all_gather | solution.py:112
  252.0 9.3 %multiply_convert_fusion.1 = (bf16[512,1408]{1,0:T(8,128)(2,1)S(1)}, bf16[512,1408]{1,0:T(8,128)(2,1)S(1)}) fusion(f32[512,2816]{1,0:T(8,128)} %copy-done.4, bf16[2048,1408]{1,0:T(8,128)(2,1)} %all-gather.8.cloned.1.call-done, bf16[128,2048]{0,1:T(8,128)(2,1)} %collective-permute-done.14, bf16[128,2048]{0,1:T(8,128)(2,1)} %collective-permute-done.13, ...), kind=kOutput, calls=%fused_computation.14 | convolution fusion | flops 2970550272 | bytes 16515072 | tf_op jit(solution)/shard_map/dot_general | solution.py:43
  261.3 10.4 %fusion.83 = (bf16[512,2048]{1,0:T(8,128)(2,1)S(1)}, f32[512,2048]{1,0:T(8,128)}) fusion(bf16[2048,2816]{1,0:T(8,128)(2,1)} %all-gather.6.cloned.1.call-done, bf16[512,1408]{1,0:T(8,128)(2,1)S(1)} %get-tuple-element.69, bf16[512,1408]{1,0:T(8,128)(2,1)S(1)} %get-tuple-element.68), kind=kOutput, calls=%fused_computation.170 | convolution fusion | flops 5912395776 | bytes 20709376 | tf_op jit(solution)/shard_map/dot_general | solution.py:47
  276.4 10.8 %convolution_convert_fusion = bf16[2048,2816]{1,0:T(8,128)(2,1)} fusion(bf16[512,1408]{1,0:T(8,128)(2,1)S(1)} %get-tuple-element.69, bf16[512,1408]{1,0:T(8,128)(2,1)S(1)} %get-tuple-element.68, bf16[128,2048]{1,0:T(8,128)(2,1)S(1)} %copy-done.47, bf16[128,2048]{1,0:T(8,128)(2,1)S(1)} %copy-done.49, bf16[128,2048]{1,0:T(8,128)(2,1)} %collective-permute-done.9, ...), kind=kOutput, calls=%fused_computation.1 | convolution fusion | flops 5925502976 | bytes 16515072 | tf_op jit(solution)/shard_map/dot_general | solution.py:51
  287.9 11.6 %collective-permute-done.17 = bf16[128,2048]{1,0:T(8,128)(2,1)S(1)} collective-permute-done((bf16[128,2048]{1,0:T(8,128)(2,1)}, bf16[128,2048]{1,0:T(8,128)(2,1)S(1)}, u32[]{:S(2)}, u32[]{:S(2)}) %collective-permute-start.17) | collective-permute-done | bytes 524320 | tf_op jit(solution)/shard_map/ppermute | solution.py:101
  302.9 14.7 %reduce-scatter.4.cloned.1.call-done = bf16[256,1408]{1,0:T(8,128)(2,1)} async-done(((bf16[2048,1408]{1,0:T(8,128)(2,1)}), bf16[256,1408]{1,0:T(8,128)(2,1)}) %reduce-scatter.4.cloned.1.call-update) | async-done | bytes 720912 | tf_op jit(solution)/shard_map/reduce_scatter | solution.py:117
  326.8 12.2 %collective-permute-done.20 = bf16[128,2048]{1,0:T(8,128)(2,1)S(1)} collective-permute-done((bf16[128,2048]{1,0:T(8,128)(2,1)S(1)}, bf16[128,2048]{1,0:T(8,128)(2,1)S(1)}, u32[]{:S(2)}, u32[]{:S(2)}) %collective-permute-start.20) | collective-permute-done | bytes 524320 | tf_op jit(solution)/shard_map/ppermute | solution.py:93
  339.0 8.2 %collective-permute-done.19 = bf16[128,2048]{1,0:T(8,128)(2,1)S(1)} collective-permute-done((bf16[128,2048]{1,0:T(8,128)(2,1)S(1)}, bf16[128,2048]{1,0:T(8,128)(2,1)S(1)}, u32[]{:S(2)}, u32[]{:S(2)}) %collective-permute-start.19) | collective-permute-done | bytes 524320 | tf_op jit(solution)/shard_map/ppermute | solution.py:93
  347.6 3.7 multiply_reduce_fusion.1
  372.6 64.9 %reduce-scatter.6.cloned.1.call-done = bf16[256,2816]{1,0:T(8,128)(2,1)} async-done(((bf16[2048,2816]{1,0:T(8,128)(2,1)}), bf16[256,2816]{1,0:T(8,128)(2,1)}) %reduce-scatter.6.cloned.1.call-update) | async-done | bytes 1441808 | tf_op jit(solution)/shard_map/reduce_scatter | solution.py:117
  439.1 6.1 %fusion.84 = (bf16[512,2048]{1,0:T(8,128)(2,1)S(1)}, f32[512,2048]{1,0:T(8,128)S(1)}) fusion(bf16[512,1408]{1,0:T(8,128)(2,1)} %copy-done.21, bf16[2048,1408]{1,0:T(8,128)(2,1)} %all-gather.8.cloned.1.call-done), kind=kOutput, calls=%fused_computation.171 | convolution fusion | flops 2953838592 | bytes 13500416 | tf_op jit(solution)/shard_map/dot_general | solution.py:47
  448.8 5.0 fusion.85
  461.6 10.7 %collective-permute-done.23 = bf16[128,2048]{1,0:T(8,128)(2,1)S(1)} collective-permute-done((bf16[128,2048]{1,0:T(8,128)(2,1)S(1)}, bf16[128,2048]{1,0:T(8,128)(2,1)S(1)}, u32[]{:S(2)}, u32[]{:S(2)}) %collective-permute-start.23) | collective-permute-done | bytes 524320 | tf_op jit(solution)/shard_map/ppermute | solution.py:101
  482.6 12.3 %collective-permute-done.26 = bf16[128,2048]{1,0:T(8,128)(2,1)} collective-permute-done((bf16[128,2048]{1,0:T(8,128)(2,1)}, bf16[128,2048]{1,0:T(8,128)(2,1)}, u32[]{:S(2)}, u32[]{:S(2)}) %collective-permute-start.26) | collective-permute-done | bytes 524320 | tf_op jit(solution)/shard_map/ppermute | solution.py:101
  494.9 4.2 collective-permute-done.25
  503.4 3.5 all-to-all-start.4
  514.8 4.9 all-to-all-done.4
  (276 shorter events, 149.5 us)
Async XLA Ops:
  7.2 75.4 %all-gather.4.cloned.1.call-start = ((), (), s32[]{:S(2)}) async-start(), calls=%async_computation.9 | async-start | bytes 5898240 | tf_op jit(solution)/shard_map/all_gather | solution.py:112
  26.7 164.3 %all-gather.6.cloned.1.call-start = ((), (), s32[]{:S(2)}) async-start(), calls=%async_computation.10 | async-start | bytes 12976128 | tf_op jit(solution)/shard_map/all_gather | solution.py:112
  50.0 21.4 %all-to-all-start.2 = ((bf16[4,64,1408]{2,1,0:T(8,128)(2,1)}), bf16[4,64,1408]{2,1,0:T(8,128)(2,1)S(1)}, u32[]{:S(2)}, u32[]{:S(2)}) async-start(bf16[4,64,1408]{2,1,0:T(8,128)(2,1)} %copy.125), calls=%async_computation.2 | async-start | bytes 1441792 | tf_op jit(solution)/shard_map/all_to_all | solution.py:109
  53.5 198.5 %all-gather.8.cloned.1.call-start = ((), (), s32[]{:S(2)}) async-start(), calls=%async_computation.11 | async-start | bytes 6488064 | tf_op jit(solution)/shard_map/all_gather | solution.py:112
  54.7 33.2 %collective-permute-start.5 = (bf16[128,2048]{1,0:T(8,128)(2,1)S(1)}, bf16[128,2048]{1,0:T(8,128)(2,1)S(1)}, u32[]{:S(2)}, u32[]{:S(2)}) collective-permute-start(bf16[128,2048]{1,0:T(8,128)(2,1)S(1)} %multiply_convert_fusion.4), channel_id=1, source_target_pairs={{0,24},{8,16},{16,8},{24,0},{1,25},{9,17},{17,9},{25,1},{2,26},{10... | collective-permute-start | bytes 1572872 | tf_op jit(solution)/shard_map/ppermute | solution.py:93
  57.6 30.8 %collective-permute-start.4 = (bf16[128,2048]{1,0:T(8,128)(2,1)S(1)}, bf16[128,2048]{1,0:T(8,128)(2,1)}, u32[]{:S(2)}, u32[]{:S(2)}) collective-permute-start(bf16[128,2048]{1,0:T(8,128)(2,1)S(1)} %multiply_convert_fusion.4), channel_id=1, source_target_pairs={{0,16},{8,24},{16,0},{24,8},{1,17},{9,25},{17,1},{25,9},{2,18},{10... | collective-permute-start | bytes 1572872 | tf_op jit(solution)/shard_map/ppermute | solution.py:93
  58.2 30.3 %collective-permute-start.3 = (bf16[128,2048]{1,0:T(8,128)(2,1)S(1)}, bf16[128,2048]{1,0:T(8,128)(2,1)}, u32[]{:S(2)}, u32[]{:S(2)}) collective-permute-start(bf16[128,2048]{1,0:T(8,128)(2,1)S(1)} %multiply_convert_fusion.4), channel_id=1, source_target_pairs={{0,8},{8,0},{16,24},{24,16},{1,9},{9,1},{17,25},{25,17},{2,10},{10... | collective-permute-start | bytes 1572872 | tf_op jit(solution)/shard_map/ppermute | solution.py:93
  72.2 245.4 %reduce-scatter.4.cloned.1.call-start = ((), (), s32[]{:S(2)}) async-start(), calls=%async_computation.12 | async-start | bytes 6488064 | tf_op jit(solution)/shard_map/reduce_scatter | solution.py:117
  111.7 15.0 %collective-permute-start.6 = (bf16[128,2048]{1,0:T(8,128)(2,1)}, bf16[128,2048]{1,0:T(8,128)(2,1)S(1)}, u32[]{:S(2)}, u32[]{:S(2)}) collective-permute-start(bf16[128,2048]{1,0:T(8,128)(2,1)} %get-tuple-element.83), channel_id=1, source_target_pairs={{0,8},{8,0},{16,24},{24,16},{1,9},{9,1},{17,25},{25,17},{2,10},{10... | collective-permute-start | bytes 1572872 | tf_op jit(solution)/shard_map/ppermute | solution.py:101
  113.2 23.9 %collective-permute-start.8 = (bf16[128,2048]{1,0:T(8,128)(2,1)}, bf16[128,2048]{1,0:T(8,128)(2,1)S(1)}, u32[]{:S(2)}, u32[]{:S(2)}) collective-permute-start(bf16[128,2048]{1,0:T(8,128)(2,1)} %get-tuple-element.84), channel_id=1, source_target_pairs={{0,24},{8,16},{16,8},{24,0},{1,25},{9,17},{17,9},{25,1},{2,26},{10... | collective-permute-start | bytes 1572872 | tf_op jit(solution)/shard_map/ppermute | solution.py:101
  114.7 23.8 %collective-permute-start.7 = (bf16[128,2048]{1,0:T(8,128)(2,1)}, bf16[128,2048]{1,0:T(8,128)(2,1)S(1)}, u32[]{:S(2)}, u32[]{:S(2)}) collective-permute-start(bf16[128,2048]{1,0:T(8,128)(2,1)} %get-tuple-element.85), channel_id=1, source_target_pairs={{0,16},{8,24},{16,0},{24,8},{1,17},{9,25},{17,1},{25,9},{2,18},{10... | collective-permute-start | bytes 1572872 | tf_op jit(solution)/shard_map/ppermute | solution.py:101
  141.4 15.8 %collective-permute-start.11 = (bf16[128,2048]{1,0:T(8,128)(2,1)S(1)}, bf16[128,2048]{1,0:T(8,128)(2,1)S(1)}, u32[]{:S(2)}, u32[]{:S(2)}) collective-permute-start(bf16[128,2048]{1,0:T(8,128)(2,1)S(1)} %multiply_convert_fusion.3), channel_id=1, source_target_pairs={{0,24},{8,16},{16,8},{24,0},{1,25},{9,17},{17,9},{25,1},{2,26},{10... | collective-permute-start | bytes 1572872 | tf_op jit(solution)/shard_map/ppermute | solution.py:93
  142.9 25.5 %collective-permute-start.10 = (bf16[128,2048]{1,0:T(8,128)(2,1)S(1)}, bf16[128,2048]{1,0:T(8,128)(2,1)S(1)}, u32[]{:S(2)}, u32[]{:S(2)}) collective-permute-start(bf16[128,2048]{1,0:T(8,128)(2,1)S(1)} %multiply_convert_fusion.3), channel_id=1, source_target_pairs={{0,16},{8,24},{16,0},{24,8},{1,17},{9,25},{17,1},{25,9},{2,18},{10... | collective-permute-start | bytes 1572872 | tf_op jit(solution)/shard_map/ppermute | solution.py:93
  144.4 24.9 %collective-permute-start.9 = (bf16[128,2048]{1,0:T(8,128)(2,1)S(1)}, bf16[128,2048]{1,0:T(8,128)(2,1)}, u32[]{:S(2)}, u32[]{:S(2)}) collective-permute-start(bf16[128,2048]{1,0:T(8,128)(2,1)S(1)} %multiply_convert_fusion.3), channel_id=1, source_target_pairs={{0,8},{8,0},{16,24},{24,16},{1,9},{9,1},{17,25},{25,17},{2,10},{10... | collective-permute-start | bytes 1572872 | tf_op jit(solution)/shard_map/ppermute | solution.py:93
  146.8 56.9 %collective-permute-start.14 = (bf16[128,2048]{0,1:T(8,128)(2,1)S(1)}, bf16[128,2048]{0,1:T(8,128)(2,1)}, u32[]{:S(2)}, u32[]{:S(2)}) collective-permute-start(bf16[128,2048]{0,1:T(8,128)(2,1)S(1)} %bitcast_convert_fusion), channel_id=1, source_target_pairs={{0,24},{8,16},{16,8},{24,0},{1,25},{9,17},{17,9},{25,1},{2,26},{10... | collective-permute-start | bytes 1572872 | tf_op jit(solution)/shard_map/ppermute | solution.py:93
  148.4 55.4 %collective-permute-start.13 = (bf16[128,2048]{0,1:T(8,128)(2,1)S(1)}, bf16[128,2048]{0,1:T(8,128)(2,1)}, u32[]{:S(2)}, u32[]{:S(2)}) collective-permute-start(bf16[128,2048]{0,1:T(8,128)(2,1)S(1)} %bitcast_convert_fusion), channel_id=1, source_target_pairs={{0,16},{8,24},{16,0},{24,8},{1,17},{9,25},{17,1},{25,9},{2,18},{10... | collective-permute-start | bytes 1572872 | tf_op jit(solution)/shard_map/ppermute | solution.py:93
  157.2 46.5 %collective-permute-start.12 = (bf16[128,2048]{0,1:T(8,128)(2,1)S(1)}, bf16[128,2048]{0,1:T(8,128)(2,1)}, u32[]{:S(2)}, u32[]{:S(2)}) collective-permute-start(bf16[128,2048]{0,1:T(8,128)(2,1)S(1)} %bitcast_convert_fusion), channel_id=1, source_target_pairs={{0,8},{8,0},{16,24},{24,16},{1,9},{9,1},{17,25},{25,17},{2,10},{10... | collective-permute-start | bytes 1572872 | tf_op jit(solution)/shard_map/ppermute | solution.py:93
  252.0 185.5 %reduce-scatter.6.cloned.1.call-start = ((), (), s32[]{:S(2)}) async-start(), calls=%async_computation.13 | async-start | bytes 12976128 | tf_op jit(solution)/shard_map/reduce_scatter | solution.py:117
  272.9 15.0 %collective-permute-start.15 = (bf16[128,2048]{1,0:T(8,128)(2,1)}, bf16[128,2048]{1,0:T(8,128)(2,1)S(1)}, u32[]{:S(2)}, u32[]{:S(2)}) collective-permute-start(bf16[128,2048]{1,0:T(8,128)(2,1)} %get-tuple-element.80), channel_id=1, source_target_pairs={{0,8},{8,0},{16,24},{24,16},{1,9},{9,1},{17,25},{25,17},{2,10},{10... | collective-permute-start | bytes 1572872 | tf_op jit(solution)/shard_map/ppermute | solution.py:101
  274.3 25.1 %collective-permute-start.17 = (bf16[128,2048]{1,0:T(8,128)(2,1)}, bf16[128,2048]{1,0:T(8,128)(2,1)S(1)}, u32[]{:S(2)}, u32[]{:S(2)}) collective-permute-start(bf16[128,2048]{1,0:T(8,128)(2,1)} %get-tuple-element.81), channel_id=1, source_target_pairs={{0,24},{8,16},{16,8},{24,0},{1,25},{9,17},{17,9},{25,1},{2,26},{10... | collective-permute-start | bytes 1572872 | tf_op jit(solution)/shard_map/ppermute | solution.py:101
  275.8 25.1 %collective-permute-start.16 = (bf16[128,2048]{1,0:T(8,128)(2,1)}, bf16[128,2048]{1,0:T(8,128)(2,1)}, u32[]{:S(2)}, u32[]{:S(2)}) collective-permute-start(bf16[128,2048]{1,0:T(8,128)(2,1)} %get-tuple-element.82), channel_id=1, source_target_pairs={{0,16},{8,24},{16,0},{24,8},{1,17},{9,25},{17,1},{25,9},{2,18},{10... | collective-permute-start | bytes 1572872 | tf_op jit(solution)/shard_map/ppermute | solution.py:101
  317.6 203.8 %reduce-scatter.8.cloned.1.call-start = ((), (), s32[]{:S(2)}) async-start(), calls=%async_computation.14 | async-start | bytes 5898240 | tf_op jit(solution)/shard_map/reduce_scatter | solution.py:117
  323.3 15.7 %collective-permute-start.20 = (bf16[128,2048]{1,0:T(8,128)(2,1)S(1)}, bf16[128,2048]{1,0:T(8,128)(2,1)S(1)}, u32[]{:S(2)}, u32[]{:S(2)}) collective-permute-start(bf16[128,2048]{1,0:T(8,128)(2,1)S(1)} %get-tuple-element.64), channel_id=1, source_target_pairs={{0,24},{8,16},{16,8},{24,0},{1,25},{9,17},{17,9},{25,1},{2,26},{10... | collective-permute-start | bytes 1572872 | tf_op jit(solution)/shard_map/ppermute | solution.py:93
  325.7 21.5 %collective-permute-start.19 = (bf16[128,2048]{1,0:T(8,128)(2,1)S(1)}, bf16[128,2048]{1,0:T(8,128)(2,1)S(1)}, u32[]{:S(2)}, u32[]{:S(2)}) collective-permute-start(bf16[128,2048]{1,0:T(8,128)(2,1)S(1)} %get-tuple-element.64), channel_id=1, source_target_pairs={{0,16},{8,24},{16,0},{24,8},{1,17},{9,25},{17,1},{25,9},{2,18},{10... | collective-permute-start | bytes 1572872 | tf_op jit(solution)/shard_map/ppermute | solution.py:93
  326.3 21.0 %collective-permute-start.18 = (bf16[128,2048]{1,0:T(8,128)(2,1)S(1)}, bf16[128,2048]{1,0:T(8,128)(2,1)S(1)}, u32[]{:S(2)}, u32[]{:S(2)}) collective-permute-start(bf16[128,2048]{1,0:T(8,128)(2,1)S(1)} %get-tuple-element.64), channel_id=1, source_target_pairs={{0,8},{8,0},{16,24},{24,16},{1,9},{9,1},{17,25},{25,17},{2,10},{10... | collective-permute-start | bytes 1572872 | tf_op jit(solution)/shard_map/ppermute | solution.py:93
  446.8 25.5 %collective-permute-start.23 = (bf16[128,2048]{1,0:T(8,128)(2,1)S(1)}, bf16[128,2048]{1,0:T(8,128)(2,1)S(1)}, u32[]{:S(2)}, u32[]{:S(2)}) collective-permute-start(bf16[128,2048]{1,0:T(8,128)(2,1)S(1)} %get-tuple-element.78), channel_id=1, source_target_pairs={{0,24},{8,16},{16,8},{24,0},{1,25},{9,17},{17,9},{25,1},{2,26},{10... | collective-permute-start | bytes 1572872 | tf_op jit(solution)/shard_map/ppermute | solution.py:101
  448.2 25.8 %collective-permute-start.22 = (bf16[128,2048]{1,0:T(8,128)(2,1)S(1)}, bf16[128,2048]{1,0:T(8,128)(2,1)S(1)}, u32[]{:S(2)}, u32[]{:S(2)}) collective-permute-start(bf16[128,2048]{1,0:T(8,128)(2,1)S(1)} %get-tuple-element.79), channel_id=1, source_target_pairs={{0,16},{8,24},{16,0},{24,8},{1,17},{9,25},{17,1},{25,9},{2,18},{10... | collective-permute-start | bytes 1572872 | tf_op jit(solution)/shard_map/ppermute | solution.py:101
  455.0 27.7 %collective-permute-start.24 = (bf16[128,2048]{1,0:T(8,128)(2,1)}, bf16[128,2048]{1,0:T(8,128)(2,1)S(1)}, u32[]{:S(2)}, u32[]{:S(2)}) collective-permute-start(bf16[128,2048]{1,0:T(8,128)(2,1)} %get-tuple-element.74), channel_id=1, source_target_pairs={{0,8},{8,0},{16,24},{24,16},{1,9},{9,1},{17,25},{25,17},{2,10},{10... | collective-permute-start | bytes 1572872 | tf_op jit(solution)/shard_map/ppermute | solution.py:101
  456.4 38.5 %collective-permute-start.26 = (bf16[128,2048]{1,0:T(8,128)(2,1)}, bf16[128,2048]{1,0:T(8,128)(2,1)}, u32[]{:S(2)}, u32[]{:S(2)}) collective-permute-start(bf16[128,2048]{1,0:T(8,128)(2,1)} %get-tuple-element.75), channel_id=1, source_target_pairs={{0,24},{8,16},{16,8},{24,0},{1,25},{9,17},{17,9},{25,1},{2,26},{10... | collective-permute-start | bytes 1572872 | tf_op jit(solution)/shard_map/ppermute | solution.py:101
  460.1 39.0 %collective-permute-start.25 = (bf16[128,2048]{1,0:T(8,128)(2,1)}, bf16[128,2048]{1,0:T(8,128)(2,1)}, u32[]{:S(2)}, u32[]{:S(2)}) collective-permute-start(bf16[128,2048]{1,0:T(8,128)(2,1)} %get-tuple-element.76), channel_id=1, source_target_pairs={{0,16},{8,24},{16,0},{24,8},{1,17},{9,25},{17,1},{25,9},{2,18},{10... | collective-permute-start | bytes 1572872 | tf_op jit(solution)/shard_map/ppermute | solution.py:101
  475.8 26.7 %all-to-all-start.5 = ((bf16[4,64,1408]{2,1,0:T(8,128)(2,1)}), bf16[4,64,1408]{2,1,0:T(8,128)(2,1)S(1)}, u32[]{:S(2)}, u32[]{:S(2)}) async-start(bf16[4,64,1408]{2,1,0:T(8,128)(2,1)} %bitcast.46), calls=%async_computation.8 | async-start | bytes 1441792 | tf_op jit(solution)/shard_map/all_to_all | solution.py:109
  503.4 16.3 %all-to-all-start.4 = ((bf16[4,64,2816]{2,1,0:T(8,128)(2,1)}), bf16[4,64,2816]{2,1,0:T(8,128)(2,1)S(1)}, u32[]{:S(2)}, u32[]{:S(2)}) async-start(bf16[4,64,2816]{2,1,0:T(8,128)(2,1)} %bitcast.153), calls=%async_computation.7 | async-start | bytes 2883584 | tf_op jit(solution)/shard_map/all_to_all | solution.py:109
  (60 other events, 484.5 us)
Sparse Core Ops, SparseCore 0:
  26.8 55.6 all-gather.3
  84.2 106.8 all-gather.5
  193.3 58.6 all-gather.7
  254.1 63.4 reduce-scatter.3
  319.7 117.6 reduce-scatter.5
  439.6 58.2 reduce-scatter.7

commit v3 on v2

--- a/solution.py
+++ b/solution.py
@@ -225,7 +225,6 @@
     query_back = rotate_back(grad_query * score_scale, cos_all[:, None, :], sin_all[:, None, :])
     grad_query_pre = query_back.reshape(seq_len, query_cols).astype(bf16)
     grad_hat_one = scattered(mm_nt(grad_query_pre, query_all)) + mm_nt(grad_kv_pre, kv_all)
-    input_grad = unpermuted(grad_middle + norm_back(grad_hat_one, hat_one, inv_one))
     attn_grad = jnp.concatenate(
         [
             mm_tn(hat_one_seq, grad_query_pre).astype(bf16),
@@ -234,7 +233,10 @@
         ],
         axis=1,
     )
-    attn_grad, ff_sum = lax.optimization_barrier((attn_grad, ff_sum))
+    attn_grad, ff_sum, grad_hat_one, layer_out = lax.optimization_barrier(
+        (attn_grad, ff_sum, grad_hat_one, layer_out)
+    )
+    input_grad = unpermuted(grad_middle + norm_back(grad_hat_one, hat_one, inv_one))
     ff_share = own_share(ff_sum)
     attn_share = own_share(summed(attn_grad))
     query_raw = joined(attn_share[:, :, :query_cols])

time: 555 us -> 528 us (0.951)
  waiting for transfers between devices: 275 us -> 246 us
    reduce_scatter x3, waiting for transfers between devices: 79.6 us -> 44.3 us  [summed(): lax.psum_scatter(grads.astype(bf16), 'fsdp', scatter_dimension=0, tiled=T...]
    all_to_all x4, waiting for transfers between devices: 19.2 us -> 26.9 us  [exchanged(): return lax.all_to_all(packed, 'dp', 0, 0)]
    unnamed x112 -> x116, local copies, waits for them, and re-layouts: 16.3 us -> 18.5 us
  transfers between devices with their start and end apart: 40 -> 40, of which waited for: 26 -> 24; matrix products, arithmetic and copies ran while one was open for 27% -> 30% of each run, Pallas kernels for 0% -> 0%
where the time goes in v3:
time: 528 us; the launch traced here: 522 us
  waiting for transfers between devices  246 us (47%)
  matrix products  92.9 us (18%)
  starting transfers between devices  50.9 us (10%)
  other arithmetic  41.3 us (8%)
  local copies, waits for them, and re-layouts  39.6 us (8%)
  blocking collectives  35.5 us (7%)
  between operations  16 us (3%)
    all_gather x3, waiting for transfers between devices, all_rows(): lax.all_gather(packed.reshape(dp_size * own_rows, packed.shape[2]), 'fsdp...  69 us
    ppermute x15, waiting for transfers between devices, scattered(): total = total + lax.ppermute(part, 'dp', peers(k)).astype(f32)  67.8 us
    reduce_scatter x3, waiting for transfers between devices, summed(): lax.psum_scatter(grads.astype(bf16), 'fsdp', scatter_dimension=0, tiled=T...  44.3 us
    ppermute x15, waiting for transfers between devices, gathered(): lax.ppermute(block, 'dp', peers(k))  37.7 us
    all_to_all x2, blocking collectives, exchanged(): return lax.all_to_all(packed, 'dp', 0, 0)  35.5 us
    dot_general x5, matrix products, mm_nt(): lax.dot_general(left, right, (((1,), (1,)), ((), ())), preferred_element_...  31.2 us
    dot_general x5, matrix products, mm(): return jnp.dot(left, right, preferred_element_type=f32)  28.2 us
    all_to_all x4, waiting for transfers between devices, exchanged(): return lax.all_to_all(packed, 'dp', 0, 0)  26.9 us
  transfers between devices with their start and end apart: 40, of which 24 were waited for; matrix products, arithmetic and copies ran while one was open for 30% of the time, Pallas kernels for 0%

profile of v3, /device:TPU:0, one launch (start us, length us, event | category | flops | bytes accessed | tf_op | source)
XLA Modules:
  0.0 522.0 jit_solution(2765041614177270195)
XLA Ops:
  11.7 15.0 %all_to_all.30 = bf16[4,64,1280]{2,1,0:T(8,128)(2,1)} all-to-all(bf16[4,64,1280]{2,1,0:T(8,128)(2,1)S(1)} %copy.116), channel_id=1, replica_groups=mesh['dp'=4,'fsdp'=8] {'dp'}, dimensions={0} | all-to-all | bytes 1310720 | tf_op jit(solution)/shard_map/all_to_all | solution.py:109
  28.3 20.5 %all_to_all.31 = bf16[4,64,2816]{2,1,0:T(8,128)(2,1)} all-to-all(bf16[4,64,2816]{2,1,0:T(8,128)(2,1)S(1)} %copy.122), channel_id=1, replica_groups=mesh['dp'=4,'fsdp'=8] {'dp'}, dimensions={0} | all-to-all | bytes 2883584 | tf_op jit(solution)/shard_map/all_to_all | solution.py:109
  58.3 13.0 %all-to-all-done.2 = bf16[4,64,1408]{2,1,0:T(8,128)(2,1)S(1)} async-done(((bf16[4,64,1408]{2,1,0:T(8,128)(2,1)}), bf16[4,64,1408]{2,1,0:T(8,128)(2,1)S(1)}, u32[]{:S(2)}, u32[]{:S(2)}) %all-to-all-start.2) | async-done | bytes 720928 | tf_op jit(solution)/shard_map/all_to_all | solution.py:109
  75.2 7.4 %all-gather.4.cloned.1.call-done = bf16[2048,1280]{1,0:T(8,128)(2,1)} async-done(((bf16[256,1280]{1,0:T(8,128)(2,1)}), bf16[2048,1280]{1,0:T(8,128)(2,1)}) %all-gather.4.cloned.1.call-update) | async-done | bytes 5242896 | tf_op jit(solution)/shard_map/all_gather | solution.py:112
  105.4 5.1 fusion.82
  117.8 8.9 %collective-permute-done.6 = bf16[128,2048]{1,0:T(8,128)(2,1)S(1)} collective-permute-done((bf16[128,2048]{1,0:T(8,128)(2,1)}, bf16[128,2048]{1,0:T(8,128)(2,1)S(1)}, u32[]{:S(2)}, u32[]{:S(2)}) %collective-permute-start.6) | collective-permute-done | bytes 524320 | tf_op jit(solution)/shard_map/ppermute | solution.py:101
  126.8 10.4 %collective-permute-done.8 = bf16[128,2048]{1,0:T(8,128)(2,1)S(1)} collective-permute-done((bf16[128,2048]{1,0:T(8,128)(2,1)}, bf16[128,2048]{1,0:T(8,128)(2,1)S(1)}, u32[]{:S(2)}, u32[]{:S(2)}) %collective-permute-start.8) | collective-permute-done | bytes 524320 | tf_op jit(solution)/shard_map/ppermute | solution.py:101
  149.8 7.4 %collective-permute-done.11 = bf16[128,2048]{1,0:T(8,128)(2,1)S(1)} collective-permute-done((bf16[128,2048]{1,0:T(8,128)(2,1)S(1)}, bf16[128,2048]{1,0:T(8,128)(2,1)S(1)}, u32[]{:S(2)}, u32[]{:S(2)}) %collective-permute-start.11) | collective-permute-done | bytes 524320 | tf_op jit(solution)/shard_map/ppermute | solution.py:93
  158.6 9.8 %collective-permute-done.10 = bf16[128,2048]{1,0:T(8,128)(2,1)S(1)} collective-permute-done((bf16[128,2048]{1,0:T(8,128)(2,1)S(1)}, bf16[128,2048]{1,0:T(8,128)(2,1)S(1)}, u32[]{:S(2)}, u32[]{:S(2)}) %collective-permute-start.10) | collective-permute-done | bytes 524320 | tf_op jit(solution)/shard_map/ppermute | solution.py:93
  169.3 21.8 %all-gather.6.cloned.1.call-done = bf16[2048,2816]{1,0:T(8,128)(2,1)} async-done(((bf16[256,2816]{1,0:T(8,128)(2,1)}), bf16[2048,2816]{1,0:T(8,128)(2,1)}) %all-gather.6.cloned.1.call-update) | async-done | bytes 11534352 | tf_op jit(solution)/shard_map/all_gather | solution.py:112
  191.1 10.1 %fusion.50 = f32[512,2816]{1,0:T(8,128)S(1)} fusion(bf16[2048,2816]{1,0:T(8,128)(2,1)} %all-gather.6.cloned.1.call-done, bf16[128,2048]{1,0:T(8,128)(2,1)} %copy-done.48, bf16[128,2048]{1,0:T(8,128)(2,1)} %copy-done.50, bf16[128,2048]{1,0:T(8,128)(2,1)} %collective-permute-done.9, bf16[128,2048]{1,0:T(8,128)(2,1)S(1)} %multiply_convert_fusion.3), kind=kOutput, calls=%fused_computation.109 | convolution fusion | flops 5913968640 | bytes 19398656 | tf_op jit(solution)/shard_map/dot_general | solution.py:43
  204.8 7.3 %convolution_convert_fusion.1 = bf16[2048,1408]{1,0:T(8,128)(2,1)} fusion(bf16[512,1408]{1,0:T(8,128)(2,1)S(1)} %multiply_convert_fusion.2, bf16[128,2048]{0,1:T(8,128)(2,1)} %collective-permute-done.14, bf16[128,2048]{0,1:T(8,128)(2,1)} %collective-permute-done.13, bf16[128,2048]{0,1:T(8,128)(2,1)} %collective-permute-done.12, ...), kind=kOutput, calls=%fused_computation.2 | convolution fusion | flops 2964062208 | bytes 9306112 | tf_op jit(solution)/shard_map/dot_general | solution.py:51
  212.1 39.8 %all-gather.8.cloned.1.call-done = bf16[2048,1408]{1,0:T(8,128)(2,1)} async-done(((bf16[256,1408]{1,0:T(8,128)(2,1)}), bf16[2048,1408]{1,0:T(8,128)(2,1)}) %all-gather.8.cloned.1.call-update) | async-done | bytes 5767184 | tf_op jit(solution)/shard_map/all_gather | solution.py:112
  252.0 9.3 %multiply_convert_fusion.1 = (bf16[512,1408]{1,0:T(8,128)(2,1)S(1)}, bf16[512,1408]{1,0:T(8,128)(2,1)S(1)}) fusion(f32[512,2816]{1,0:T(8,128)} %copy-done.4, bf16[2048,1408]{1,0:T(8,128)(2,1)} %all-gather.8.cloned.1.call-done, bf16[128,2048]{0,1:T(8,128)(2,1)} %collective-permute-done.14, bf16[128,2048]{0,1:T(8,128)(2,1)} %collective-permute-done.13, ...), kind=kOutput, calls=%fused_computation.14 | convolution fusion | flops 2970550272 | bytes 16515072 | tf_op jit(solution)/shard_map/dot_general | solution.py:43
  261.3 10.8 %fusion.83 = (bf16[512,2048]{1,0:T(8,128)(2,1)S(1)}, f32[512,2048]{1,0:T(8,128)}) fusion(bf16[2048,2816]{1,0:T(8,128)(2,1)} %all-gather.6.cloned.1.call-done, bf16[512,1408]{1,0:T(8,128)(2,1)S(1)} %get-tuple-element.73, bf16[512,1408]{1,0:T(8,128)(2,1)S(1)} %get-tuple-element.72), kind=kOutput, calls=%fused_computation.170 | convolution fusion | flops 5912395776 | bytes 20709376 | tf_op jit(solution)/shard_map/dot_general | solution.py:47
  276.8 10.8 %convolution_convert_fusion = bf16[2048,2816]{1,0:T(8,128)(2,1)} fusion(bf16[512,1408]{1,0:T(8,128)(2,1)S(1)} %get-tuple-element.73, bf16[512,1408]{1,0:T(8,128)(2,1)S(1)} %get-tuple-element.72, bf16[128,2048]{1,0:T(8,128)(2,1)S(1)} %copy-done.49, bf16[128,2048]{1,0:T(8,128)(2,1)S(1)} %copy-done.51, bf16[128,2048]{1,0:T(8,128)(2,1)} %collective-permute-done.9, ...), kind=kOutput, calls=%fused_computation.1 | convolution fusion | flops 5925502976 | bytes 16515072 | tf_op jit(solution)/shard_map/dot_general | solution.py:51
  288.3 11.6 %collective-permute-done.17 = bf16[128,2048]{1,0:T(8,128)(2,1)S(1)} collective-permute-done((bf16[128,2048]{1,0:T(8,128)(2,1)}, bf16[128,2048]{1,0:T(8,128)(2,1)S(1)}, u32[]{:S(2)}, u32[]{:S(2)}) %collective-permute-start.17) | collective-permute-done | bytes 524320 | tf_op jit(solution)/shard_map/ppermute | solution.py:101
  303.4 14.2 %reduce-scatter.4.cloned.1.call-done = bf16[256,1408]{1,0:T(8,128)(2,1)} async-done(((bf16[2048,1408]{1,0:T(8,128)(2,1)}), bf16[256,1408]{1,0:T(8,128)(2,1)}) %reduce-scatter.4.cloned.1.call-update) | async-done | bytes 720912 | tf_op jit(solution)/shard_map/reduce_scatter | solution.py:117
  326.4 12.2 %collective-permute-done.20 = bf16[128,2048]{1,0:T(8,128)(2,1)S(1)} collective-permute-done((bf16[128,2048]{1,0:T(8,128)(2,1)S(1)}, bf16[128,2048]{1,0:T(8,128)(2,1)S(1)}, u32[]{:S(2)}, u32[]{:S(2)}) %collective-permute-start.20) | collective-permute-done | bytes 524320 | tf_op jit(solution)/shard_map/ppermute | solution.py:93
  338.6 8.2 %collective-permute-done.19 = bf16[128,2048]{1,0:T(8,128)(2,1)S(1)} collective-permute-done((bf16[128,2048]{1,0:T(8,128)(2,1)S(1)}, bf16[128,2048]{1,0:T(8,128)(2,1)S(1)}, u32[]{:S(2)}, u32[]{:S(2)}) %collective-permute-start.19) | collective-permute-done | bytes 524320 | tf_op jit(solution)/shard_map/ppermute | solution.py:93
  347.2 3.8 multiply_reduce_fusion.1
  363.7 7.9 %fusion.85 = (bf16[512,2048]{1,0:T(8,128)(2,1)S(1)}, f32[512,2048]{1,0:T(8,128)}) fusion(bf16[512,1408]{1,0:T(8,128)(2,1)S(1)} %copy-done.21, bf16[2048,1408]{1,0:T(8,128)(2,1)} %all-gather.8.cloned.1.call-done), kind=kOutput, calls=%fused_computation.172 | convolution fusion | flops 2953838592 | bytes 13500416 | tf_op jit(solution)/shard_map/dot_general | solution.py:47
  378.2 5.0 fusion.84
  395.2 4.8 collective-permute-done.29
  400.1 11.3 %collective-permute-done.28 = bf16[128,2048]{1,0:T(8,128)(2,1)} collective-permute-done((bf16[128,2048]{1,0:T(8,128)(2,1)}, bf16[128,2048]{1,0:T(8,128)(2,1)}, u32[]{:S(2)}, u32[]{:S(2)}) %collective-permute-start.28) | collective-permute-done | bytes 524320 | tf_op jit(solution)/shard_map/ppermute | solution.py:101
  414.5 6.4 %collective-permute-done.26 = bf16[128,2048]{1,0:T(8,128)(2,1)} collective-permute-done((bf16[128,2048]{1,0:T(8,128)(2,1)}, bf16[128,2048]{1,0:T(8,128)(2,1)}, u32[]{:S(2)}, u32[]{:S(2)}) %collective-permute-start.26) | collective-permute-done | bytes 524320 | tf_op jit(solution)/shard_map/ppermute | solution.py:101
  420.9 10.8 %collective-permute-done.25 = bf16[128,2048]{1,0:T(8,128)(2,1)S(1)} collective-permute-done((bf16[128,2048]{1,0:T(8,128)(2,1)}, bf16[128,2048]{1,0:T(8,128)(2,1)S(1)}, u32[]{:S(2)}, u32[]{:S(2)}) %collective-permute-start.25) | collective-permute-done | bytes 524320 | tf_op jit(solution)/shard_map/ppermute | solution.py:101
  437.5 3.7 all-to-all-start.5
  442.7 6.8 %all-to-all-done.5 = bf16[4,64,1408]{2,1,0:T(8,128)(2,1)S(1)} async-done(((bf16[4,64,1408]{2,1,0:T(8,128)(2,1)}), bf16[4,64,1408]{2,1,0:T(8,128)(2,1)S(1)}, u32[]{:S(2)}, u32[]{:S(2)}) %all-to-all-start.5) | async-done | bytes 720928 | tf_op jit(solution)/shard_map/all_to_all | solution.py:109
  464.1 5.3 %all-to-all-done.4 = bf16[4,64,2816]{2,1,0:T(8,128)(2,1)S(1)} async-done(((bf16[4,64,2816]{2,1,0:T(8,128)(2,1)}), bf16[4,64,2816]{2,1,0:T(8,128)(2,1)S(1)}, u32[]{:S(2)}, u32[]{:S(2)}) %all-to-all-start.4) | async-done | bytes 1441824 | tf_op jit(solution)/shard_map/all_to_all | solution.py:109
  471.3 26.7 %reduce-scatter.8.cloned.1.call-done = bf16[256,1280]{0,1:T(8,128)(2,1)} async-done(((bf16[2048,1280]{0,1:T(8,128)(2,1)}), bf16[256,1280]{0,1:T(8,128)(2,1)}) %reduce-scatter.8.cloned.1.call-update) | async-done | bytes 655376 | tf_op jit(solution)/shard_map/reduce_scatter | solution.py:117
  500.1 3.7 all-to-all-start.3
  (281 shorter events, 156.3 us)
Async XLA Ops:
  7.2 75.4 %all-gather.4.cloned.1.call-start = ((), (), s32[]{:S(2)}) async-start(), calls=%async_computation.9 | async-start | bytes 5898240 | tf_op jit(solution)/shard_map/all_gather | solution.py:112
  26.7 164.3 %all-gather.6.cloned.1.call-start = ((), (), s32[]{:S(2)}) async-start(), calls=%async_computation.10 | async-start | bytes 12976128 | tf_op jit(solution)/shard_map/all_gather | solution.py:112
  50.0 21.4 %all-to-all-start.2 = ((bf16[4,64,1408]{2,1,0:T(8,128)(2,1)}), bf16[4,64,1408]{2,1,0:T(8,128)(2,1)S(1)}, u32[]{:S(2)}, u32[]{:S(2)}) async-start(bf16[4,64,1408]{2,1,0:T(8,128)(2,1)} %copy.125), calls=%async_computation.2 | async-start | bytes 1441792 | tf_op jit(solution)/shard_map/all_to_all | solution.py:109
  53.5 198.4 %all-gather.8.cloned.1.call-start = ((), (), s32[]{:S(2)}) async-start(), calls=%async_computation.11 | async-start | bytes 6488064 | tf_op jit(solution)/shard_map/all_gather | solution.py:112
  54.8 33.1 %collective-permute-start.2 = (bf16[128,2048]{1,0:T(8,128)(2,1)S(1)}, bf16[128,2048]{1,0:T(8,128)(2,1)S(1)}, u32[]{:S(2)}, u32[]{:S(2)}) collective-permute-start(bf16[128,2048]{1,0:T(8,128)(2,1)S(1)} %multiply_convert_fusion.4), channel_id=1, source_target_pairs={{0,24},{8,16},{16,8},{24,0},{1,25},{9,17},{17,9},{25,1},{2,26},{10... | collective-permute-start | bytes 1572872 | tf_op jit(solution)/shard_map/ppermute | solution.py:93
  57.7 30.8 %collective-permute-start.1 = (bf16[128,2048]{1,0:T(8,128)(2,1)S(1)}, bf16[128,2048]{1,0:T(8,128)(2,1)}, u32[]{:S(2)}, u32[]{:S(2)}) collective-permute-start(bf16[128,2048]{1,0:T(8,128)(2,1)S(1)} %multiply_convert_fusion.4), channel_id=1, source_target_pairs={{0,16},{8,24},{16,0},{24,8},{1,17},{9,25},{17,1},{25,9},{2,18},{10... | collective-permute-start | bytes 1572872 | tf_op jit(solution)/shard_map/ppermute | solution.py:93
  58.2 30.2 %collective-permute-start = (bf16[128,2048]{1,0:T(8,128)(2,1)S(1)}, bf16[128,2048]{1,0:T(8,128)(2,1)}, u32[]{:S(2)}, u32[]{:S(2)}) collective-permute-start(bf16[128,2048]{1,0:T(8,128)(2,1)S(1)} %multiply_convert_fusion.4), channel_id=1, source_target_pairs={{0,8},{8,0},{16,24},{24,16},{1,9},{9,1},{17,25},{25,17},{2,10},{10... | collective-permute-start | bytes 1572872 | tf_op jit(solution)/shard_map/ppermute | solution.py:93
  72.2 245.3 %reduce-scatter.4.cloned.1.call-start = ((), (), s32[]{:S(2)}) async-start(), calls=%async_computation.12 | async-start | bytes 6488064 | tf_op jit(solution)/shard_map/reduce_scatter | solution.py:117
  113.2 23.9 %collective-permute-start.8 = (bf16[128,2048]{1,0:T(8,128)(2,1)}, bf16[128,2048]{1,0:T(8,128)(2,1)S(1)}, u32[]{:S(2)}, u32[]{:S(2)}) collective-permute-start(bf16[128,2048]{1,0:T(8,128)(2,1)} %get-tuple-element.88), channel_id=1, source_target_pairs={{0,24},{8,16},{16,8},{24,0},{1,25},{9,17},{17,9},{25,1},{2,26},{10... | collective-permute-start | bytes 1572872 | tf_op jit(solution)/shard_map/ppermute | solution.py:101
  114.7 23.8 %collective-permute-start.7 = (bf16[128,2048]{1,0:T(8,128)(2,1)}, bf16[128,2048]{1,0:T(8,128)(2,1)S(1)}, u32[]{:S(2)}, u32[]{:S(2)}) collective-permute-start(bf16[128,2048]{1,0:T(8,128)(2,1)} %get-tuple-element.89), channel_id=1, source_target_pairs={{0,16},{8,24},{16,0},{24,8},{1,17},{9,25},{17,1},{25,9},{2,18},{10... | collective-permute-start | bytes 1572872 | tf_op jit(solution)/shard_map/ppermute | solution.py:101
  141.4 15.8 %collective-permute-start.11 = (bf16[128,2048]{1,0:T(8,128)(2,1)S(1)}, bf16[128,2048]{1,0:T(8,128)(2,1)S(1)}, u32[]{:S(2)}, u32[]{:S(2)}) collective-permute-start(bf16[128,2048]{1,0:T(8,128)(2,1)S(1)} %multiply_convert_fusion.3), channel_id=1, source_target_pairs={{0,24},{8,16},{16,8},{24,0},{1,25},{9,17},{17,9},{25,1},{2,26},{10... | collective-permute-start | bytes 1572872 | tf_op jit(solution)/shard_map/ppermute | solution.py:93
  142.9 25.5 %collective-permute-start.10 = (bf16[128,2048]{1,0:T(8,128)(2,1)S(1)}, bf16[128,2048]{1,0:T(8,128)(2,1)S(1)}, u32[]{:S(2)}, u32[]{:S(2)}) collective-permute-start(bf16[128,2048]{1,0:T(8,128)(2,1)S(1)} %multiply_convert_fusion.3), channel_id=1, source_target_pairs={{0,16},{8,24},{16,0},{24,8},{1,17},{9,25},{17,1},{25,9},{2,18},{10... | collective-permute-start | bytes 1572872 | tf_op jit(solution)/shard_map/ppermute | solution.py:93
  144.4 24.9 %collective-permute-start.9 = (bf16[128,2048]{1,0:T(8,128)(2,1)S(1)}, bf16[128,2048]{1,0:T(8,128)(2,1)}, u32[]{:S(2)}, u32[]{:S(2)}) collective-permute-start(bf16[128,2048]{1,0:T(8,128)(2,1)S(1)} %multiply_convert_fusion.3), channel_id=1, source_target_pairs={{0,8},{8,0},{16,24},{24,16},{1,9},{9,1},{17,25},{25,17},{2,10},{10... | collective-permute-start | bytes 1572872 | tf_op jit(solution)/shard_map/ppermute | solution.py:93
  146.8 56.9 %collective-permute-start.14 = (bf16[128,2048]{0,1:T(8,128)(2,1)S(1)}, bf16[128,2048]{0,1:T(8,128)(2,1)}, u32[]{:S(2)}, u32[]{:S(2)}) collective-permute-start(bf16[128,2048]{0,1:T(8,128)(2,1)S(1)} %bitcast_convert_fusion), channel_id=1, source_target_pairs={{0,24},{8,16},{16,8},{24,0},{1,25},{9,17},{17,9},{25,1},{2,26},{10... | collective-permute-start | bytes 1572872 | tf_op jit(solution)/shard_map/ppermute | solution.py:93
  148.4 55.4 %collective-permute-start.13 = (bf16[128,2048]{0,1:T(8,128)(2,1)S(1)}, bf16[128,2048]{0,1:T(8,128)(2,1)}, u32[]{:S(2)}, u32[]{:S(2)}) collective-permute-start(bf16[128,2048]{0,1:T(8,128)(2,1)S(1)} %bitcast_convert_fusion), channel_id=1, source_target_pairs={{0,16},{8,24},{16,0},{24,8},{1,17},{9,25},{17,1},{25,9},{2,18},{10... | collective-permute-start | bytes 1572872 | tf_op jit(solution)/shard_map/ppermute | solution.py:93
  157.2 46.5 %collective-permute-start.12 = (bf16[128,2048]{0,1:T(8,128)(2,1)S(1)}, bf16[128,2048]{0,1:T(8,128)(2,1)}, u32[]{:S(2)}, u32[]{:S(2)}) collective-permute-start(bf16[128,2048]{0,1:T(8,128)(2,1)S(1)} %bitcast_convert_fusion), channel_id=1, source_target_pairs={{0,8},{8,0},{16,24},{24,16},{1,9},{9,1},{17,25},{25,17},{2,10},{10... | collective-permute-start | bytes 1572872 | tf_op jit(solution)/shard_map/ppermute | solution.py:93
  252.0 185.5 %reduce-scatter.6.cloned.1.call-start = ((), (), s32[]{:S(2)}) async-start(), calls=%async_computation.13 | async-start | bytes 12976128 | tf_op jit(solution)/shard_map/reduce_scatter | solution.py:117
  274.8 25.1 %collective-permute-start.17 = (bf16[128,2048]{1,0:T(8,128)(2,1)}, bf16[128,2048]{1,0:T(8,128)(2,1)S(1)}, u32[]{:S(2)}, u32[]{:S(2)}) collective-permute-start(bf16[128,2048]{1,0:T(8,128)(2,1)} %get-tuple-element.85), channel_id=1, source_target_pairs={{0,24},{8,16},{16,8},{24,0},{1,25},{9,17},{17,9},{25,1},{2,26},{10... | collective-permute-start | bytes 1572872 | tf_op jit(solution)/shard_map/ppermute | solution.py:101
  276.2 25.1 %collective-permute-start.16 = (bf16[128,2048]{1,0:T(8,128)(2,1)}, bf16[128,2048]{1,0:T(8,128)(2,1)}, u32[]{:S(2)}, u32[]{:S(2)}) collective-permute-start(bf16[128,2048]{1,0:T(8,128)(2,1)} %get-tuple-element.86), channel_id=1, source_target_pairs={{0,16},{8,24},{16,0},{24,8},{1,17},{9,25},{17,1},{25,9},{2,18},{10... | collective-permute-start | bytes 1572872 | tf_op jit(solution)/shard_map/ppermute | solution.py:101
  317.6 180.4 %reduce-scatter.8.cloned.1.call-start = ((), (), s32[]{:S(2)}) async-start(), calls=%async_computation.14 | async-start | bytes 5898240 | tf_op jit(solution)/shard_map/reduce_scatter | solution.py:117
  325.3 21.5 %collective-permute-start.19 = (bf16[128,2048]{1,0:T(8,128)(2,1)S(1)}, bf16[128,2048]{1,0:T(8,128)(2,1)S(1)}, u32[]{:S(2)}, u32[]{:S(2)}) collective-permute-start(bf16[128,2048]{1,0:T(8,128)(2,1)S(1)} %get-tuple-element.68), channel_id=1, source_target_pairs={{0,16},{8,24},{16,0},{24,8},{1,17},{9,25},{17,1},{25,9},{2,18},{10... | collective-permute-start | bytes 1572872 | tf_op jit(solution)/shard_map/ppermute | solution.py:93
  325.9 21.1 %collective-permute-start.18 = (bf16[128,2048]{1,0:T(8,128)(2,1)S(1)}, bf16[128,2048]{1,0:T(8,128)(2,1)S(1)}, u32[]{:S(2)}, u32[]{:S(2)}) collective-permute-start(bf16[128,2048]{1,0:T(8,128)(2,1)S(1)} %get-tuple-element.68), channel_id=1, source_target_pairs={{0,8},{8,0},{16,24},{24,16},{1,9},{9,1},{17,25},{25,17},{2,10},{10... | collective-permute-start | bytes 1572872 | tf_op jit(solution)/shard_map/ppermute | solution.py:93
  360.1 26.6 %collective-permute-start.21 = (bf16[128,256]{1,0:T(8,128)(2,1)S(1)}, bf16[128,256]{1,0:T(8,128)(2,1)S(1)}, u32[]{:S(2)}, u32[]{:S(2)}) collective-permute-start(bf16[128,256]{1,0:T(8,128)(2,1)S(1)} %get-tuple-element.106), channel_id=1, source_target_pairs={{0,8},{8,0},{16,24},{24,16},{1,9},{9,1},{17,25},{25,17},{2,10},{10... | collective-permute-start | bytes 196616 | tf_op jit(solution)/shard_map/ppermute | solution.py:101
  361.7 25.8 %collective-permute-start.23 = (bf16[128,256]{1,0:T(8,128)(2,1)S(1)}, bf16[128,256]{1,0:T(8,128)(2,1)S(1)}, u32[]{:S(2)}, u32[]{:S(2)}) collective-permute-start(bf16[128,256]{1,0:T(8,128)(2,1)S(1)} %get-tuple-element.107), channel_id=1, source_target_pairs={{0,24},{8,16},{16,8},{24,0},{1,25},{9,17},{17,9},{25,1},{2,26},{10... | collective-permute-start | bytes 196616 | tf_op jit(solution)/shard_map/ppermute | solution.py:101
  363.1 25.9 %collective-permute-start.22 = (bf16[128,256]{1,0:T(8,128)(2,1)S(1)}, bf16[128,256]{1,0:T(8,128)(2,1)S(1)}, u32[]{:S(2)}, u32[]{:S(2)}) collective-permute-start(bf16[128,256]{1,0:T(8,128)(2,1)S(1)} %get-tuple-element.108), channel_id=1, source_target_pairs={{0,16},{8,24},{16,0},{24,8},{1,17},{9,25},{17,1},{25,9},{2,18},{10... | collective-permute-start | bytes 196616 | tf_op jit(solution)/shard_map/ppermute | solution.py:101
  372.8 21.9 %collective-permute-start.27 = (bf16[128,2048]{1,0:T(8,128)(2,1)}, bf16[128,2048]{1,0:T(8,128)(2,1)}, u32[]{:S(2)}, u32[]{:S(2)}) collective-permute-start(bf16[128,2048]{1,0:T(8,128)(2,1)} %get-tuple-element.78), channel_id=1, source_target_pairs={{0,8},{8,0},{16,24},{24,16},{1,9},{9,1},{17,25},{25,17},{2,10},{10... | collective-permute-start | bytes 1572872 | tf_op jit(solution)/shard_map/ppermute | solution.py:101
  374.3 25.8 %collective-permute-start.29 = (bf16[128,2048]{1,0:T(8,128)(2,1)}, bf16[128,2048]{1,0:T(8,128)(2,1)}, u32[]{:S(2)}, u32[]{:S(2)}) collective-permute-start(bf16[128,2048]{1,0:T(8,128)(2,1)} %get-tuple-element.79), channel_id=1, source_target_pairs={{0,24},{8,16},{16,8},{24,0},{1,25},{9,17},{17,9},{25,1},{2,26},{10... | collective-permute-start | bytes 1572872 | tf_op jit(solution)/shard_map/ppermute | solution.py:101
  386.8 24.6 %collective-permute-start.28 = (bf16[128,2048]{1,0:T(8,128)(2,1)}, bf16[128,2048]{1,0:T(8,128)(2,1)}, u32[]{:S(2)}, u32[]{:S(2)}) collective-permute-start(bf16[128,2048]{1,0:T(8,128)(2,1)} %get-tuple-element.80), channel_id=1, source_target_pairs={{0,16},{8,24},{16,0},{24,8},{1,17},{9,25},{17,1},{25,9},{2,18},{10... | collective-permute-start | bytes 1572872 | tf_op jit(solution)/shard_map/ppermute | solution.py:101
  387.5 27.0 %collective-permute-start.24 = (bf16[128,2048]{1,0:T(8,128)(2,1)}, bf16[128,2048]{1,0:T(8,128)(2,1)}, u32[]{:S(2)}, u32[]{:S(2)}) collective-permute-start(bf16[128,2048]{1,0:T(8,128)(2,1)} %get-tuple-element.81), channel_id=1, source_target_pairs={{0,8},{8,0},{16,24},{24,16},{1,9},{9,1},{17,25},{25,17},{2,10},{10... | collective-permute-start | bytes 1572872 | tf_op jit(solution)/shard_map/ppermute | solution.py:101
  389.0 31.9 %collective-permute-start.26 = (bf16[128,2048]{1,0:T(8,128)(2,1)}, bf16[128,2048]{1,0:T(8,128)(2,1)}, u32[]{:S(2)}, u32[]{:S(2)}) collective-permute-start(bf16[128,2048]{1,0:T(8,128)(2,1)} %get-tuple-element.82), channel_id=1, source_target_pairs={{0,24},{8,16},{16,8},{24,0},{1,25},{9,17},{17,9},{25,1},{2,26},{10... | collective-permute-start | bytes 1572872 | tf_op jit(solution)/shard_map/ppermute | solution.py:101
  394.6 37.0 %collective-permute-start.25 = (bf16[128,2048]{1,0:T(8,128)(2,1)}, bf16[128,2048]{1,0:T(8,128)(2,1)S(1)}, u32[]{:S(2)}, u32[]{:S(2)}) collective-permute-start(bf16[128,2048]{1,0:T(8,128)(2,1)} %get-tuple-element.83), channel_id=1, source_target_pairs={{0,16},{8,24},{16,0},{24,8},{1,17},{9,25},{17,1},{25,9},{2,18},{10... | collective-permute-start | bytes 1572872 | tf_op jit(solution)/shard_map/ppermute | solution.py:101
  450.4 19.1 %all-to-all-start.4 = ((bf16[4,64,2816]{2,1,0:T(8,128)(2,1)}), bf16[4,64,2816]{2,1,0:T(8,128)(2,1)S(1)}, u32[]{:S(2)}, u32[]{:S(2)}) async-start(bf16[4,64,2816]{2,1,0:T(8,128)(2,1)} %bitcast.154), calls=%async_computation.7 | async-start | bytes 2883584 | tf_op jit(solution)/shard_map/all_to_all | solution.py:109
  (62 other events, 505.8 us)
Sparse Core Ops, SparseCore 0:
  26.8 55.6 all-gather.3
  84.2 106.8 all-gather.5
  193.3 58.6 all-gather.7
  254.1 63.4 reduce-scatter.3
  319.7 117.6 reduce-scatter.5
  439.6 58.2 reduce-scatter.7

commit v4 on v3

--- a/solution.py
+++ b/solution.py
@@ -119,6 +119,35 @@
     def own_share(share):
         return exchanged(share.reshape(dp_size, own_rows, share.shape[1])).astype(f32)
 
+    pair_cols = head_width // (2 * dp_size)
+
+    def kv_split(matrix):
+        rows = matrix.shape[0]
+        keys = matrix[:, :head_width].reshape(rows, 2, dp_size, pair_cols)
+        vals = matrix[:, head_width:].reshape(rows, dp_size, 2 * pair_cols)
+        keys = keys.transpose(2, 0, 1, 3).reshape(dp_size, rows, 2 * pair_cols)
+        return jnp.concatenate([keys, vals.transpose(1, 0, 2)], axis=2)
+
+    def kv_join(blocks):
+        rows = blocks.shape[1]
+        keys = blocks[:, :, : 2 * pair_cols].reshape(dp_size, rows, 2, pair_cols)
+        keys = keys.transpose(1, 2, 0, 3).reshape(rows, head_width)
+        vals = blocks[:, :, 2 * pair_cols :].transpose(1, 0, 2).reshape(rows, head_width)
+        return jnp.concatenate([keys, vals], axis=1)
+
+    def flipped(parts):
+        parts = list(parts)
+        for bit in [1 << j for j in range(dp_size.bit_length() - 1)]:
+            flip = (dp_index & bit) != 0
+            parts = [jnp.where(flip, parts[k ^ bit], parts[k]) for k in range(dp_size)]
+        return parts
+
+    def moved_rows(block, k):
+        rows = block.shape[0] // dp_size
+        return jnp.concatenate(
+            [block[(k ^ m) * rows : (k ^ m) * rows + rows] for m in range(dp_size)], axis=0
+        )
+
     def joined(blocks):
         return blocks.transpose(1, 0, 2).reshape(own_rows, dp_size * blocks.shape[2])
 
@@ -131,8 +160,8 @@
     attn_pack = jnp.concatenate(
         [
             column_blocks(scaled(query_weight, gain_one)),
-            jnp.broadcast_to(scaled(kv_weight, gain_one)[None], (dp_size, own_rows, kv_width)),
             column_blocks(out_weight),
+            kv_split(scaled(kv_weight, gain_one)),
         ],
         axis=2,
     )
@@ -147,15 +176,16 @@
     ff_all = all_rows(exchanged(ff_pack))
     down_all = all_rows(exchanged(column_blocks(down_weight)))
     query_all = attn_all[:, :query_cols]
-    kv_all = attn_all[:, query_cols : query_cols + kv_width]
-    out_all = attn_all[:, query_cols + kv_width :]
+    out_all = attn_all[:, query_cols : 2 * query_cols]
+    kv_all = attn_all[:, 2 * query_cols :]
 
     def block_positions(k):
         return (dp_index ^ k) * tok_rows + jnp.arange(tok_rows, dtype=jnp.int32)
 
     positions = jnp.concatenate([block_positions(k) for k in range(dp_size)])
     cos_all, sin_all = rope_tables(positions, head_width // 2)
-    cos_own, sin_own = cos_all[:tok_rows], sin_all[:tok_rows]
+    cos_own = lax.dynamic_slice_in_dim(cos_all, dp_index * pair_cols, pair_cols, axis=1)
+    sin_own = lax.dynamic_slice_in_dim(sin_all, dp_index * pair_cols, pair_cols, axis=1)
     seq_len = positions.shape[0]
 
     inputs = permuted(tokens[0]).astype(f32)
@@ -163,10 +193,14 @@
     hat_one = inputs * inv_one
     hat_one_low = hat_one.astype(bf16)
     hat_one_seq = gathered(hat_one_low)
-    kv_pre = mm(hat_one_low, kv_all)
-    key_rot = rotate(kv_pre[:, :head_width], cos_own, sin_own)
-    shared = jnp.concatenate([key_rot, kv_pre[:, head_width:]], axis=1).astype(bf16)
-    shared_seq = gathered(shared)
+    kv_pre = mm(hat_one_seq, kv_all)
+    key_rot = rotate(kv_pre[:, : 2 * pair_cols], cos_own, sin_own)
+    shared_cols = jnp.concatenate([key_rot, kv_pre[:, 2 * pair_cols :]], axis=1).astype(bf16)
+    shared_parts = [shared_cols]
+    for k in range(1, dp_size):
+        shared_parts.append(moved_rows(lax.ppermute(shared_cols, "dp", peers(k)), k))
+    shared_seq = kv_join(jnp.stack(flipped(shared_parts)))
+    shared = shared_seq[:tok_rows]
     keys, values = shared_seq[:, :head_width], shared_seq[:, head_width:]
     query_pre = mm(hat_one_seq, query_all).reshape(seq_len, head_count, head_width)
     query_rot = rotate(query_pre, cos_all[:, None, :], sin_all[:, None, :])
@@ -193,6 +227,11 @@
     seq_weight = jnp.sum(jnp.where(group_ids == seq_group[0], group_weight, 0.0))
     grad_out = permuted(out_grad[0]).astype(f32) * seq_weight
     grad_out_seq = gathered(grad_out.astype(bf16))
+    late_parts = flipped(kv_split(kv_grad[0]))
+    late_parts = late_parts[:1] + [
+        lax.ppermute(late_parts[k], "dp", peers(k)) for k in range(1, dp_size)
+    ]
+    kv_late = jnp.concatenate(late_parts, axis=0).astype(f32)
     down_grad = mm_tn(grad_out_seq, hidden).astype(bf16)
     down_all, down_grad = lax.optimization_barrier((down_all, down_grad))
     down_sum = summed(down_grad)
@@ -218,30 +257,33 @@
     grad_query = jnp.einsum("htk,kd->thd", grad_scores, keys, preferred_element_type=f32)
     grad_keys = jnp.einsum("htk,thd->kd", grad_scores, queries, preferred_element_type=f32)
     grad_values = jnp.einsum("htk,thd->kd", probs_low, grad_heads, preferred_element_type=f32)
-    kv_total = scattered(jnp.concatenate([grad_keys, grad_values], axis=1))
-    kv_total = kv_total + kv_grad[0].astype(f32)
-    key_back = rotate_back(kv_total[:, :head_width], cos_own, sin_own)
-    grad_kv_pre = jnp.concatenate([key_back, kv_total[:, head_width:]], axis=1).astype(bf16)
+    kv_parts = flipped(kv_split(jnp.concatenate([grad_keys, grad_values], axis=1)))
+    kv_total = kv_parts[0] + kv_late
+    for k in range(1, dp_size):
+        part = moved_rows(kv_parts[k].astype(bf16), k)
+        kv_total = kv_total + lax.ppermute(part, "dp", peers(k)).astype(f32)
+    key_back = rotate_back(kv_total[:, : 2 * pair_cols], cos_own, sin_own)
+    grad_kv_pre = jnp.concatenate([key_back, kv_total[:, 2 * pair_cols :]], axis=1).astype(bf16)
     query_back = rotate_back(grad_query * score_scale, cos_all[:, None, :], sin_all[:, None, :])
     grad_query_pre = query_back.reshape(seq_len, query_cols).astype(bf16)
-    grad_hat_one = scattered(mm_nt(grad_query_pre, query_all)) + mm_nt(grad_kv_pre, kv_all)
+    grad_hat_one = mm_nt(grad_query_pre, query_all) + mm_nt(grad_kv_pre, kv_all)
     attn_grad = jnp.concatenate(
         [
             mm_tn(hat_one_seq, grad_query_pre).astype(bf16),
-            mm_tn(hat_one_low, grad_kv_pre).astype(bf16),
             mm_tn(grad_mid_seq, attn_rows).astype(bf16),
+            mm_tn(hat_one_seq, grad_kv_pre).astype(bf16),
         ],
         axis=1,
     )
     attn_grad, ff_sum, grad_hat_one, layer_out = lax.optimization_barrier(
         (attn_grad, ff_sum, grad_hat_one, layer_out)
     )
-    input_grad = unpermuted(grad_middle + norm_back(grad_hat_one, hat_one, inv_one))
+    input_grad = unpermuted(grad_middle + norm_back(scattered(grad_hat_one), hat_one, inv_one))
     ff_share = own_share(ff_sum)
     attn_share = own_share(summed(attn_grad))
     query_raw = joined(attn_share[:, :, :query_cols])
-    kv_raw = jnp.sum(attn_share[:, :, query_cols : query_cols + kv_width], axis=0)
-    out_weight_grad = joined(attn_share[:, :, query_cols + kv_width :])
+    out_weight_grad = joined(attn_share[:, :, query_cols : 2 * query_cols])
+    kv_raw = kv_join(attn_share[:, :, 2 * query_cols :])
     gate_raw = joined(ff_share[:, :, :ff_cols])
     up_raw = joined(ff_share[:, :, ff_cols:])
 

time: 528 us -> 515 us (0.975)
  waiting for transfers between devices: 246 us -> 212 us
  local copies, waits for them, and re-layouts: 39.6 us -> 48.5 us
  starting transfers between devices: 50.9 us -> 58.5 us
    all_gather x3, waiting for transfers between devices: 69 us -> 54.7 us  [all_rows(): lax.all_gather(packed.reshape(dp_size * own_rows, packed.shape[2]), 'fsdp...]
    ppermute x15 -> x12, waiting for transfers between devices: 67.8 us -> 54.9 us  [scattered(): total = total + lax.ppermute(part, 'dp', peers(k)).astype(f32)]
    ppermute x0 -> x9, starting transfers between devices: none -> 11.6 us  [the longest x3 4.38 us: local(): lax.ppermute(late_parts[k], 'dp', peers(k))]
    ppermute x15 -> x12, starting transfers between devices: 18.5 us -> 13.2 us  [gathered(): lax.ppermute(block, 'dp', peers(k))]
    ppermute x15 -> x12, waiting for transfers between devices: 37.7 us -> 33.5 us  [gathered(): lax.ppermute(block, 'dp', peers(k))]
    ppermute x15 -> x12, starting transfers between devices: 17.6 us -> 14.2 us  [scattered(): total = total + lax.ppermute(part, 'dp', peers(k)).astype(f32)]
    unnamed x116 -> x142, local copies, waits for them, and re-layouts: 18.5 us -> 21.8 us
  transfers between devices with their start and end apart: 40 -> 43, of which waited for: 24 -> 24; matrix products, arithmetic and copies ran while one was open for 30% -> 33% of each run, Pallas kernels for 0% -> 0%
where the time goes in v4:
time: 515 us; the launch traced here: 509 us
  waiting for transfers between devices  212 us (41%)
  matrix products  93.2 us (18%)
  starting transfers between devices  58.5 us (11%)
  local copies, waits for them, and re-layouts  48.5 us (9%)
  other arithmetic  45 us (9%)
  blocking collectives  35.1 us (7%)
  between operations  16.4 us (3%)
    ppermute x12, waiting for transfers between devices, scattered(): total = total + lax.ppermute(part, 'dp', peers(k)).astype(f32)  54.9 us
    all_gather x3, waiting for transfers between devices, all_rows(): lax.all_gather(packed.reshape(dp_size * own_rows, packed.shape[2]), 'fsdp...  54.7 us
    reduce_scatter x3, waiting for transfers between devices, summed(): lax.psum_scatter(grads.astype(bf16), 'fsdp', scatter_dimension=0, tiled=T...  40.8 us
    all_to_all x2, blocking collectives, exchanged(): return lax.all_to_all(packed, 'dp', 0, 0)  35.1 us
    ppermute x12, waiting for transfers between devices, gathered(): lax.ppermute(block, 'dp', peers(k))  33.5 us
    dot_general x5, matrix products, mm_nt(): lax.dot_general(left, right, (((1,), (1,)), ((), ())), preferred_element_...  31.4 us
    dot_general x5, matrix products, mm(): return jnp.dot(left, right, preferred_element_type=f32)  29.3 us
    all_to_all x4, waiting for transfers between devices, exchanged(): return lax.all_to_all(packed, 'dp', 0, 0)  28 us
  transfers between devices with their start and end apart: 43, of which 24 were waited for; matrix products, arithmetic and copies ran while one was open for 33% of the time, Pallas kernels for 0%

profile of v4, /device:TPU:0, one launch (start us, length us, event | category | flops | bytes accessed | tf_op | source)
XLA Modules:
  0.0 508.6 jit_solution(5568478676565913725)
XLA Ops:
  11.6 14.5 %all_to_all.30 = bf16[4,64,1088]{2,1,0:T(8,128)(2,1)} all-to-all(bf16[4,64,1088]{2,1,0:T(8,128)(2,1)S(1)} %concatenate.196), channel_id=1, replica_groups=mesh['dp'=4,'fsdp'=8] {'dp'}, dimensions={0} | all-to-all | bytes 1114112 | tf_op jit(solution)/shard_map/all_to_all | solution.py:109
  27.7 20.6 %all_to_all.31 = bf16[4,64,2816]{2,1,0:T(8,128)(2,1)} all-to-all(bf16[4,64,2816]{2,1,0:T(8,128)(2,1)S(1)} %copy.171), channel_id=1, replica_groups=mesh['dp'=4,'fsdp'=8] {'dp'}, dimensions={0} | all-to-all | bytes 2883584 | tf_op jit(solution)/shard_map/all_to_all | solution.py:109
  61.0 19.7 %all-to-all-done.2 = bf16[4,64,1408]{2,1,0:T(8,128)(2,1)S(1)} async-done(((bf16[4,64,1408]{2,1,0:T(8,128)(2,1)}), bf16[4,64,1408]{2,1,0:T(8,128)(2,1)S(1)}, u32[]{:S(2)}, u32[]{:S(2)}) %all-to-all-start.2) | async-done | bytes 720928 | tf_op jit(solution)/shard_map/all_to_all | solution.py:109
  87.8 3.6 fusion.16
  99.2 3.5 fusion.89
  107.2 5.1 %fusion.91 = (bf16[512,2048]{1,0:T(8,128)(2,1)S(1)}, f32[512,2048]{1,0:T(8,128)}) fusion(bf16[512,512]{0,1:T(8,128)(2,1)S(1)} %bitcast.244, bf16[2048,1088]{1,0:T(8,128)(2,1)} %all-gather.4.cloned.1.call-done), kind=kOutput, calls=%fused_computation.232 | convolution fusion | flops 1074790400 | bytes 8912896 | tf_op jit(solution)/shard_map/dot_general | solution.py:47
  119.6 9.8 %collective-permute-done.8 = bf16[128,2048]{1,0:T(8,128)(2,1)S(1)} collective-permute-done((bf16[128,2048]{1,0:T(8,128)(2,1)}, bf16[128,2048]{1,0:T(8,128)(2,1)S(1)}, u32[]{:S(2)}, u32[]{:S(2)}) %collective-permute-start.8) | collective-permute-done | bytes 524320 | tf_op jit(solution)/shard_map/ppermute | solution.py:101
  129.5 9.5 %collective-permute-done.7 = bf16[128,2048]{1,0:T(8,128)(2,1)S(1)} collective-permute-done((bf16[128,2048]{1,0:T(8,128)(2,1)}, bf16[128,2048]{1,0:T(8,128)(2,1)S(1)}, u32[]{:S(2)}, u32[]{:S(2)}) %collective-permute-start.7) | collective-permute-done | bytes 524320 | tf_op jit(solution)/shard_map/ppermute | solution.py:101
  150.2 8.3 %collective-permute-done.11 = bf16[128,2048]{1,0:T(8,128)(2,1)S(1)} collective-permute-done((bf16[128,2048]{1,0:T(8,128)(2,1)S(1)}, bf16[128,2048]{1,0:T(8,128)(2,1)S(1)}, u32[]{:S(2)}, u32[]{:S(2)}) %collective-permute-start.11) | collective-permute-done | bytes 524320 | tf_op jit(solution)/shard_map/ppermute | solution.py:93
  159.0 10.8 %collective-permute-done.10 = bf16[128,2048]{1,0:T(8,128)(2,1)S(1)} collective-permute-done((bf16[128,2048]{1,0:T(8,128)(2,1)S(1)}, bf16[128,2048]{1,0:T(8,128)(2,1)S(1)}, u32[]{:S(2)}, u32[]{:S(2)}) %collective-permute-start.10) | collective-permute-done | bytes 524320 | tf_op jit(solution)/shard_map/ppermute | solution.py:93
  170.6 14.9 %all-gather.6.cloned.1.call-done = bf16[2048,2816]{1,0:T(8,128)(2,1)} async-done(((bf16[256,2816]{1,0:T(8,128)(2,1)}), bf16[2048,2816]{1,0:T(8,128)(2,1)}) %all-gather.6.cloned.1.call-update) | async-done | bytes 11534352 | tf_op jit(solution)/shard_map/all_gather | solution.py:112
  185.5 10.1 %fusion.48 = f32[512,2816]{1,0:T(8,128)S(1)} fusion(bf16[2048,2816]{1,0:T(8,128)(2,1)} %all-gather.6.cloned.1.call-done, bf16[128,2048]{1,0:T(8,128)(2,1)} %copy-done.57, bf16[128,2048]{1,0:T(8,128)(2,1)} %copy-done.59, bf16[128,2048]{1,0:T(8,128)(2,1)} %collective-permute-done.9, bf16[128,2048]{1,0:T(8,128)(2,1)S(1)} %multiply_convert_fusion.3), kind=kOutput, calls=%fused_computation.106 | convolution fusion | flops 5913968640 | bytes 19398656 | tf_op jit(solution)/shard_map/dot_general | solution.py:43
  199.3 7.2 %convolution_convert_fusion.1 = bf16[2048,1408]{1,0:T(8,128)(2,1)} fusion(bf16[512,1408]{1,0:T(8,128)(2,1)S(1)} %multiply_convert_fusion.2, bf16[128,2048]{0,1:T(8,128)(2,1)} %collective-permute-done.14, bf16[128,2048]{0,1:T(8,128)(2,1)} %collective-permute-done.13, bf16[128,2048]{0,1:T(8,128)(2,1)} %collective-permute-done.12, ...), kind=kOutput, calls=%fused_computation.2 | convolution fusion | flops 2964062208 | bytes 9306112 | tf_op jit(solution)/shard_map/dot_general | solution.py:51
  206.5 39.8 %all-gather.8.cloned.1.call-done = bf16[2048,1408]{1,0:T(8,128)(2,1)} async-done(((bf16[256,1408]{1,0:T(8,128)(2,1)}), bf16[2048,1408]{1,0:T(8,128)(2,1)}) %all-gather.8.cloned.1.call-update) | async-done | bytes 5767184 | tf_op jit(solution)/shard_map/all_gather | solution.py:112
  246.4 9.3 %multiply_convert_fusion.1 = (bf16[512,1408]{1,0:T(8,128)(2,1)S(1)}, bf16[512,1408]{1,0:T(8,128)(2,1)S(1)}) fusion(f32[512,2816]{1,0:T(8,128)} %copy-done.3, bf16[2048,1408]{1,0:T(8,128)(2,1)} %all-gather.8.cloned.1.call-done, bf16[128,2048]{0,1:T(8,128)(2,1)} %collective-permute-done.14, bf16[128,2048]{0,1:T(8,128)(2,1)} %collective-permute-done.13, ...), kind=kOutput, calls=%fused_computation.15 | convolution fusion | flops 2970550272 | bytes 16515072 | tf_op jit(solution)/shard_map/dot_general | solution.py:43
  255.7 10.8 %fusion.92 = (bf16[512,2048]{1,0:T(8,128)(2,1)S(1)}, f32[512,2048]{1,0:T(8,128)}) fusion(bf16[2048,2816]{1,0:T(8,128)(2,1)} %all-gather.6.cloned.1.call-done, bf16[512,1408]{1,0:T(8,128)(2,1)S(1)} %get-tuple-element.83, bf16[512,1408]{1,0:T(8,128)(2,1)S(1)} %get-tuple-element.82), kind=kOutput, calls=%fused_computation.233 | convolution fusion | flops 5912395776 | bytes 20709376 | tf_op jit(solution)/shard_map/dot_general | solution.py:47
  271.3 10.8 %convolution_convert_fusion = bf16[2048,2816]{1,0:T(8,128)(2,1)} fusion(bf16[512,1408]{1,0:T(8,128)(2,1)S(1)} %get-tuple-element.83, bf16[512,1408]{1,0:T(8,128)(2,1)S(1)} %get-tuple-element.82, bf16[128,2048]{1,0:T(8,128)(2,1)S(1)} %copy-done.58, bf16[128,2048]{1,0:T(8,128)(2,1)S(1)} %copy-done.60, bf16[128,2048]{1,0:T(8,128)(2,1)} %collective-permute-done.9, ...), kind=kOutput, calls=%fused_computation.1 | convolution fusion | flops 5925502976 | bytes 16515072 | tf_op jit(solution)/shard_map/dot_general | solution.py:51
  283.7 10.5 %collective-permute-done.16 = bf16[128,2048]{1,0:T(8,128)(2,1)S(1)} collective-permute-done((bf16[128,2048]{1,0:T(8,128)(2,1)}, bf16[128,2048]{1,0:T(8,128)(2,1)S(1)}, u32[]{:S(2)}, u32[]{:S(2)}) %collective-permute-start.16) | collective-permute-done | bytes 524320 | tf_op jit(solution)/shard_map/ppermute | solution.py:101
  297.0 15.0 %reduce-scatter.4.cloned.1.call-done = bf16[256,1408]{1,0:T(8,128)(2,1)} async-done(((bf16[2048,1408]{1,0:T(8,128)(2,1)}), bf16[256,1408]{1,0:T(8,128)(2,1)}) %reduce-scatter.4.cloned.1.call-update) | async-done | bytes 720912 | tf_op jit(solution)/shard_map/reduce_scatter | solution.py:117
  328.1 7.1 %collective-permute-done.20 = bf16[128,2048]{1,0:T(8,128)(2,1)S(1)} collective-permute-done((bf16[128,2048]{1,0:T(8,128)(2,1)}, bf16[128,2048]{1,0:T(8,128)(2,1)S(1)}, u32[]{:S(2)}, u32[]{:S(2)}) %collective-permute-start.20) | collective-permute-done | bytes 524320 | tf_op jit(solution)/shard_map/ppermute | solution.py:93
  336.7 7.0 %collective-permute-done.19 = bf16[128,2048]{1,0:T(8,128)(2,1)S(1)} collective-permute-done((bf16[128,2048]{1,0:T(8,128)(2,1)}, bf16[128,2048]{1,0:T(8,128)(2,1)S(1)}, u32[]{:S(2)}, u32[]{:S(2)}) %collective-permute-start.19) | collective-permute-done | bytes 524320 | tf_op jit(solution)/shard_map/ppermute | solution.py:93
  345.4 4.1 multiply_reduce_fusion.1
  362.6 5.1 fusion.14
  370.5 5.2 %fusion.93 = (bf16[512,2048]{1,0:T(8,128)(2,1)S(1)}, f32[512,2048]{1,0:T(8,128)}) fusion(bf16[512,1408]{1,0:T(8,128)(2,1)S(1)} %copy-done.18, bf16[2048,1408]{1,0:T(8,128)(2,1)S(1)} %bitcast.288), kind=kOutput, calls=%fused_computation.234 | convolution fusion | flops 2953838592 | bytes 13500416 | tf_op jit(solution)/shard_map/dot_general | solution.py:47
  389.0 5.2 %convolution_add_fusion = f32[512,2048]{1,0:T(8,128)} fusion(f32[512,2048]{1,0:T(8,128)} %fusion.14, bf16[2048,1088]{1,0:T(8,128)(2,1)} %all-gather.4.cloned.1.call-done, bf16[512,32]{0,1:T(8,128)(2,1)S(1)} %slice.475, bf16[512,16]{0,1:T(8,128)(2,1)S(1)} %get-tuple-element.115, bf16[512,16]{0,1:T(8,128)(2,1)S(1)} %get-tuple-element.114), kind=kOutput, calls=%fused_computation.10 | convolution fusion | flops 135462912 | bytes 8978432 | tf_op jit(solution)/shard_map/dot_general | solution.py:47
  395.5 9.4 %collective-permute-done.28 = bf16[128,2048]{1,0:T(8,128)(2,1)} collective-permute-done((bf16[128,2048]{1,0:T(8,128)(2,1)}, bf16[128,2048]{1,0:T(8,128)(2,1)}, u32[]{:S(2)}, u32[]{:S(2)}) %collective-permute-start.28) | collective-permute-done | bytes 524320 | tf_op jit(solution)/shard_map/ppermute | solution.py:101
  407.2 24.7 %reduce-scatter.6.cloned.1.call-done = bf16[256,2816]{1,0:T(8,128)(2,1)} async-done(((bf16[2048,2816]{1,0:T(8,128)(2,1)}), bf16[256,2816]{1,0:T(8,128)(2,1)}) %reduce-scatter.6.cloned.1.call-update) | async-done | bytes 1441808 | tf_op jit(solution)/shard_map/reduce_scatter | solution.py:117
  431.9 3.8 all-to-all-start.5
  443.9 4.0 all-to-all-done.5
  450.2 8.0 %all-to-all-start.4 = ((bf16[4,64,2816]{2,1,0:T(8,128)(2,1)}), bf16[4,64,2816]{2,1,0:T(8,128)(2,1)S(1)}, u32[]{:S(2)}, u32[]{:S(2)}) async-start(bf16[4,64,2816]{2,1,0:T(8,128)(2,1)} %bitcast.254), calls=%async_computation.7 | async-start | bytes 2883584 | tf_op jit(solution)/shard_map/all_to_all | solution.py:109
  459.5 11.0 %collective-permute-done.31 = bf16[128,2048]{1,0:T(8,128)(2,1)} collective-permute-done((bf16[128,2048]{1,0:T(8,128)(2,1)}, bf16[128,2048]{1,0:T(8,128)(2,1)}, u32[]{:S(2)}, u32[]{:S(2)}) %collective-permute-start.31) | collective-permute-done | bytes 524320 | tf_op jit(solution)/shard_map/ppermute | solution.py:101
  487.1 3.6 all-to-all-start.3
  (343 shorter events, 160.1 us)
Async XLA Ops:
  7.2 74.7 %all-gather.4.cloned.1.call-start = ((), (), s32[]{:S(2)}) async-start(), calls=%async_computation.9 | async-start | bytes 5308416 | tf_op jit(solution)/shard_map/all_gather | solution.py:112
  26.1 159.4 %all-gather.6.cloned.1.call-start = ((), (), s32[]{:S(2)}) async-start(), calls=%async_computation.10 | async-start | bytes 12976128 | tf_op jit(solution)/shard_map/all_gather | solution.py:112
  49.6 32.2 %collective-permute-start.2 = (bf16[128,2048]{1,0:T(8,128)(2,1)S(1)}, bf16[128,2048]{1,0:T(8,128)(2,1)}, u32[]{:S(2)}, u32[]{:S(2)}) collective-permute-start(bf16[128,2048]{1,0:T(8,128)(2,1)S(1)} %multiply_convert_fusion.4), channel_id=1, source_target_pairs={{0,24},{8,16},{16,8},{24,0},{1,25},{9,17},{17,9},{25,1},{2,26},{10... | collective-permute-start | bytes 1572872 | tf_op jit(solution)/shard_map/ppermute | solution.py:93
  50.6 31.3 %collective-permute-start.1 = (bf16[128,2048]{1,0:T(8,128)(2,1)S(1)}, bf16[128,2048]{1,0:T(8,128)(2,1)}, u32[]{:S(2)}, u32[]{:S(2)}) collective-permute-start(bf16[128,2048]{1,0:T(8,128)(2,1)S(1)} %multiply_convert_fusion.4), channel_id=1, source_target_pairs={{0,16},{8,24},{16,0},{24,8},{1,17},{9,25},{17,1},{25,9},{2,18},{10... | collective-permute-start | bytes 1572872 | tf_op jit(solution)/shard_map/ppermute | solution.py:93
  52.1 29.8 %collective-permute-start = (bf16[128,2048]{1,0:T(8,128)(2,1)S(1)}, bf16[128,2048]{1,0:T(8,128)(2,1)}, u32[]{:S(2)}, u32[]{:S(2)}) collective-permute-start(bf16[128,2048]{1,0:T(8,128)(2,1)S(1)} %multiply_convert_fusion.4), channel_id=1, source_target_pairs={{0,8},{8,0},{16,24},{24,16},{1,9},{9,1},{17,25},{25,17},{2,10},{10... | collective-permute-start | bytes 1572872 | tf_op jit(solution)/shard_map/ppermute | solution.py:93
  54.3 26.4 %all-to-all-start.2 = ((bf16[4,64,1408]{2,1,0:T(8,128)(2,1)}), bf16[4,64,1408]{2,1,0:T(8,128)(2,1)S(1)}, u32[]{:S(2)}, u32[]{:S(2)}) async-start(bf16[4,64,1408]{2,1,0:T(8,128)(2,1)} %copy.174), calls=%async_computation.2 | async-start | bytes 1441792 | tf_op jit(solution)/shard_map/all_to_all | solution.py:109
  57.8 188.6 %all-gather.8.cloned.1.call-start = ((), (), s32[]{:S(2)}) async-start(), calls=%async_computation.11 | async-start | bytes 6488064 | tf_op jit(solution)/shard_map/all_gather | solution.py:112
  81.6 230.4 %reduce-scatter.4.cloned.1.call-start = ((), (), s32[]{:S(2)}) async-start(), calls=%async_computation.12 | async-start | bytes 6488064 | tf_op jit(solution)/shard_map/reduce_scatter | solution.py:117
  115.5 23.5 %collective-permute-start.7 = (bf16[128,2048]{1,0:T(8,128)(2,1)}, bf16[128,2048]{1,0:T(8,128)(2,1)S(1)}, u32[]{:S(2)}, u32[]{:S(2)}) collective-permute-start(bf16[128,2048]{1,0:T(8,128)(2,1)} %get-tuple-element.99), channel_id=1, source_target_pairs={{0,16},{8,24},{16,0},{24,8},{1,17},{9,25},{17,1},{25,9},{2,18},{10... | collective-permute-start | bytes 1572872 | tf_op jit(solution)/shard_map/ppermute | solution.py:101
  116.5 22.7 %collective-permute-start.6 = (bf16[128,2048]{1,0:T(8,128)(2,1)}, bf16[128,2048]{1,0:T(8,128)(2,1)S(1)}, u32[]{:S(2)}, u32[]{:S(2)}) collective-permute-start(bf16[128,2048]{1,0:T(8,128)(2,1)} %get-tuple-element.97), channel_id=1, source_target_pairs={{0,8},{8,0},{16,24},{24,16},{1,9},{9,1},{17,25},{25,17},{2,10},{10... | collective-permute-start | bytes 1572872 | tf_op jit(solution)/shard_map/ppermute | solution.py:101
  144.0 25.8 %collective-permute-start.10 = (bf16[128,2048]{1,0:T(8,128)(2,1)S(1)}, bf16[128,2048]{1,0:T(8,128)(2,1)S(1)}, u32[]{:S(2)}, u32[]{:S(2)}) collective-permute-start(bf16[128,2048]{1,0:T(8,128)(2,1)S(1)} %multiply_convert_fusion.3), channel_id=1, source_target_pairs={{0,16},{8,24},{16,0},{24,8},{1,17},{9,25},{17,1},{25,9},{2,18},{10... | collective-permute-start | bytes 1572872 | tf_op jit(solution)/shard_map/ppermute | solution.py:93
  144.8 25.8 %collective-permute-start.9 = (bf16[128,2048]{1,0:T(8,128)(2,1)S(1)}, bf16[128,2048]{1,0:T(8,128)(2,1)}, u32[]{:S(2)}, u32[]{:S(2)}) collective-permute-start(bf16[128,2048]{1,0:T(8,128)(2,1)S(1)} %multiply_convert_fusion.3), channel_id=1, source_target_pairs={{0,8},{8,0},{16,24},{24,16},{1,9},{9,1},{17,25},{25,17},{2,10},{10... | collective-permute-start | bytes 1572872 | tf_op jit(solution)/shard_map/ppermute | solution.py:93
  148.1 50.1 %collective-permute-start.14 = (bf16[128,2048]{0,1:T(8,128)(2,1)S(1)}, bf16[128,2048]{0,1:T(8,128)(2,1)}, u32[]{:S(2)}, u32[]{:S(2)}) collective-permute-start(bf16[128,2048]{0,1:T(8,128)(2,1)S(1)} %bitcast_convert_fusion), channel_id=1, source_target_pairs={{0,24},{8,16},{16,8},{24,0},{1,25},{9,17},{17,9},{25,1},{2,26},{10... | collective-permute-start | bytes 1572872 | tf_op jit(solution)/shard_map/ppermute | solution.py:93
  149.4 48.8 %collective-permute-start.13 = (bf16[128,2048]{0,1:T(8,128)(2,1)S(1)}, bf16[128,2048]{0,1:T(8,128)(2,1)}, u32[]{:S(2)}, u32[]{:S(2)}) collective-permute-start(bf16[128,2048]{0,1:T(8,128)(2,1)S(1)} %bitcast_convert_fusion), channel_id=1, source_target_pairs={{0,16},{8,24},{16,0},{24,8},{1,17},{9,25},{17,1},{25,9},{2,18},{10... | collective-permute-start | bytes 1572872 | tf_op jit(solution)/shard_map/ppermute | solution.py:93
  158.5 39.7 %collective-permute-start.12 = (bf16[128,2048]{0,1:T(8,128)(2,1)S(1)}, bf16[128,2048]{0,1:T(8,128)(2,1)}, u32[]{:S(2)}, u32[]{:S(2)}) collective-permute-start(bf16[128,2048]{0,1:T(8,128)(2,1)S(1)} %bitcast_convert_fusion), channel_id=1, source_target_pairs={{0,8},{8,0},{16,24},{24,16},{1,9},{9,1},{17,25},{25,17},{2,10},{10... | collective-permute-start | bytes 1572872 | tf_op jit(solution)/shard_map/ppermute | solution.py:93
  246.4 185.5 %reduce-scatter.6.cloned.1.call-start = ((), (), s32[]{:S(2)}) async-start(), calls=%async_computation.13 | async-start | bytes 12976128 | tf_op jit(solution)/shard_map/reduce_scatter | solution.py:117
  270.1 24.1 %collective-permute-start.16 = (bf16[128,2048]{1,0:T(8,128)(2,1)}, bf16[128,2048]{1,0:T(8,128)(2,1)S(1)}, u32[]{:S(2)}, u32[]{:S(2)}) collective-permute-start(bf16[128,2048]{1,0:T(8,128)(2,1)} %get-tuple-element.96), channel_id=1, source_target_pairs={{0,16},{8,24},{16,0},{24,8},{1,17},{9,25},{17,1},{25,9},{2,18},{10... | collective-permute-start | bytes 1572872 | tf_op jit(solution)/shard_map/ppermute | solution.py:101
  270.7 23.7 %collective-permute-start.15 = (bf16[128,2048]{1,0:T(8,128)(2,1)}, bf16[128,2048]{1,0:T(8,128)(2,1)}, u32[]{:S(2)}, u32[]{:S(2)}) collective-permute-start(bf16[128,2048]{1,0:T(8,128)(2,1)} %get-tuple-element.94), channel_id=1, source_target_pairs={{0,8},{8,0},{16,24},{24,16},{1,9},{9,1},{17,25},{25,17},{2,10},{10... | collective-permute-start | bytes 1572872 | tf_op jit(solution)/shard_map/ppermute | solution.py:101
  312.0 172.9 %reduce-scatter.8.cloned.1.call-start = ((), (), s32[]{:S(2)}) async-start(), calls=%async_computation.14 | async-start | bytes 5013504 | tf_op jit(solution)/shard_map/reduce_scatter | solution.py:117
  321.7 22.0 %collective-permute-start.19 = (bf16[128,2048]{1,0:T(8,128)(2,1)}, bf16[128,2048]{1,0:T(8,128)(2,1)S(1)}, u32[]{:S(2)}, u32[]{:S(2)}) collective-permute-start(bf16[128,2048]{1,0:T(8,128)(2,1)} %get-tuple-element.78), channel_id=1, source_target_pairs={{0,16},{8,24},{16,0},{24,8},{1,17},{9,25},{17,1},{25,9},{2,18},{10... | collective-permute-start | bytes 1572872 | tf_op jit(solution)/shard_map/ppermute | solution.py:93
  322.2 21.7 %collective-permute-start.18 = (bf16[128,2048]{1,0:T(8,128)(2,1)}, bf16[128,2048]{1,0:T(8,128)(2,1)}, u32[]{:S(2)}, u32[]{:S(2)}) collective-permute-start(bf16[128,2048]{1,0:T(8,128)(2,1)} %get-tuple-element.78), channel_id=1, source_target_pairs={{0,8},{8,0},{16,24},{24,16},{1,9},{9,1},{17,25},{25,17},{2,10},{10... | collective-permute-start | bytes 1572872 | tf_op jit(solution)/shard_map/ppermute | solution.py:93
  323.5 53.5 %collective-permute-start.23 = (bf16[128,64]{0,1:T(8,128)(2,1)}, bf16[128,64]{0,1:T(8,128)(2,1)}, u32[]{:S(2)}, u32[]{:S(2)}) collective-permute-start(bf16[128,64]{0,1:T(8,128)(2,1)} %get-tuple-element.124), channel_id=1, source_target_pairs={{0,24},{8,16},{16,8},{24,0},{1,25},{9,17},{17,9},{25,1},{2,26},{10... | collective-permute-start | bytes 49160 | tf_op jit(solution)/shard_map/ppermute | solution.py:232
  325.8 53.5 %collective-permute-start.22 = (bf16[128,64]{0,1:T(8,128)(2,1)}, bf16[128,64]{0,1:T(8,128)(2,1)}, u32[]{:S(2)}, u32[]{:S(2)}) collective-permute-start(bf16[128,64]{0,1:T(8,128)(2,1)} %get-tuple-element.123), channel_id=1, source_target_pairs={{0,16},{8,24},{16,0},{24,8},{1,17},{9,25},{17,1},{25,9},{2,18},{10... | collective-permute-start | bytes 49160 | tf_op jit(solution)/shard_map/ppermute | solution.py:232
  335.2 45.6 %collective-permute-start.21 = (bf16[128,64]{0,1:T(8,128)(2,1)}, bf16[128,64]{0,1:T(8,128)(2,1)}, u32[]{:S(2)}, u32[]{:S(2)}) collective-permute-start(bf16[128,64]{0,1:T(8,128)(2,1)} %get-tuple-element.122), channel_id=1, source_target_pairs={{0,8},{8,0},{16,24},{24,16},{1,9},{9,1},{17,25},{25,17},{2,10},{10... | collective-permute-start | bytes 49160 | tf_op jit(solution)/shard_map/ppermute | solution.py:232
  354.4 27.5 %collective-permute-start.26 = (bf16[512,64]{0,1:T(8,128)(2,1)}, bf16[512,64]{0,1:T(8,128)(2,1)}, u32[]{:S(2)}, u32[]{:S(2)}) collective-permute-start(bf16[512,64]{0,1:T(8,128)(2,1)} %pad_maximum_fusion.25), channel_id=1, source_target_pairs={{0,24},{8,16},{16,8},{24,0},{1,25},{9,17},{17,9},{25,1},{2,26},{10... | collective-permute-start | bytes 196616 | tf_op jit(solution)/shard_map/ppermute | solution.py:264
  356.7 26.3 %collective-permute-start.25 = (bf16[512,64]{0,1:T(8,128)(2,1)}, bf16[512,64]{0,1:T(8,128)(2,1)}, u32[]{:S(2)}, u32[]{:S(2)}) collective-permute-start(bf16[512,64]{0,1:T(8,128)(2,1)} %pad_maximum_fusion.24), channel_id=1, source_target_pairs={{0,16},{8,24},{16,0},{24,8},{1,17},{9,25},{17,1},{25,9},{2,18},{10... | collective-permute-start | bytes 196616 | tf_op jit(solution)/shard_map/ppermute | solution.py:264
  380.8 24.1 %collective-permute-start.28 = (bf16[128,2048]{1,0:T(8,128)(2,1)}, bf16[128,2048]{1,0:T(8,128)(2,1)}, u32[]{:S(2)}, u32[]{:S(2)}) collective-permute-start(bf16[128,2048]{1,0:T(8,128)(2,1)} %get-tuple-element.93), channel_id=1, source_target_pairs={{0,16},{8,24},{16,0},{24,8},{1,17},{9,25},{17,1},{25,9},{2,18},{10... | collective-permute-start | bytes 1572872 | tf_op jit(solution)/shard_map/ppermute | solution.py:101
  381.9 23.0 %collective-permute-start.27 = (bf16[128,2048]{1,0:T(8,128)(2,1)}, bf16[128,2048]{1,0:T(8,128)(2,1)}, u32[]{:S(2)}, u32[]{:S(2)}) collective-permute-start(bf16[128,2048]{1,0:T(8,128)(2,1)} %get-tuple-element.91), channel_id=1, source_target_pairs={{0,8},{8,0},{16,24},{24,16},{1,9},{9,1},{17,25},{25,17},{2,10},{10... | collective-permute-start | bytes 1572872 | tf_op jit(solution)/shard_map/ppermute | solution.py:101
  440.3 19.2 %collective-permute-start.32 = (bf16[128,2048]{1,0:T(8,128)(2,1)}, bf16[128,2048]{1,0:T(8,128)(2,1)}, u32[]{:S(2)}, u32[]{:S(2)}) collective-permute-start(bf16[128,2048]{1,0:T(8,128)(2,1)} %get-tuple-element.89), channel_id=1, source_target_pairs={{0,24},{8,16},{16,8},{24,0},{1,25},{9,17},{17,9},{25,1},{2,26},{10... | collective-permute-start | bytes 1572872 | tf_op jit(solution)/shard_map/ppermute | solution.py:101
  443.3 27.1 %collective-permute-start.31 = (bf16[128,2048]{1,0:T(8,128)(2,1)}, bf16[128,2048]{1,0:T(8,128)(2,1)}, u32[]{:S(2)}, u32[]{:S(2)}) collective-permute-start(bf16[128,2048]{1,0:T(8,128)(2,1)} %get-tuple-element.90), channel_id=1, source_target_pairs={{0,16},{8,24},{16,0},{24,8},{1,17},{9,25},{17,1},{25,9},{2,18},{10... | collective-permute-start | bytes 1572872 | tf_op jit(solution)/shard_map/ppermute | solution.py:101
  443.9 26.6 %collective-permute-start.30 = (bf16[128,2048]{1,0:T(8,128)(2,1)}, bf16[128,2048]{1,0:T(8,128)(2,1)}, u32[]{:S(2)}, u32[]{:S(2)}) collective-permute-start(bf16[128,2048]{1,0:T(8,128)(2,1)} %get-tuple-element.88), channel_id=1, source_target_pairs={{0,8},{8,0},{16,24},{24,16},{1,9},{9,1},{17,25},{25,17},{2,10},{10... | collective-permute-start | bytes 1572872 | tf_op jit(solution)/shard_map/ppermute | solution.py:101
  450.2 31.8 %all-to-all-start.4 = ((bf16[4,64,2816]{2,1,0:T(8,128)(2,1)}), bf16[4,64,2816]{2,1,0:T(8,128)(2,1)S(1)}, u32[]{:S(2)}, u32[]{:S(2)}) async-start(bf16[4,64,2816]{2,1,0:T(8,128)(2,1)} %bitcast.254), calls=%async_computation.7 | async-start | bytes 2883584 | tf_op jit(solution)/shard_map/all_to_all | solution.py:109
  (76 other events, 622.9 us)
Sparse Core Ops, SparseCore 0:
  26.2 50.7 all-gather.3
  78.6 106.7 all-gather.5
  187.7 58.6 all-gather.7
  248.5 63.4 reduce-scatter.3
  314.1 117.6 reduce-scatter.5
  434.0 50.8 reduce-scatter.7
